TPU v7x, 256 devices: a whole 4x4x8 slice. The times are simulated.
256 devices in a mesh: cell: 64 (over z, x, y_lo), net: 4 (over y_hi, core).
Axes of the slice: x: 4, y: 4 (y_hi: 2, y_lo: 2; y = y_hi * 2 + y_lo), z: 8, core: 2. Of those that a mesh axis runs over, the one named last changes fastest.
Arguments:
- cell_feat: bfloat16 [32768, 256], P('cell'), may hold values from -6 to 6
- out_grad: bfloat16 [32768, 256], P('cell'), may hold values from -6 to 6
- w_in: bfloat16 [256, 1024], replicated, may hold values from -0.25 to 0.25
- w_net: bfloat16 [256, 1024], replicated, may hold values from -0.25 to 0.25
- bias: float32 [1024], replicated, may hold values from -3 to 3
- w_out: bfloat16 [1024, 256], replicated, may hold values from -0.1875 to 0.1875
- send_idx: int32 [64, 64, 16], P('cell'), may hold values from 0 to 511
- pin_net: int32 [64, 4, 2, 512], P('cell', 'net'), may hold values from 0 to 127
- pin_ref: int32 [64, 4, 2, 512], P('cell', 'net'), may hold values from 0 to 1535
- block_count: int32 [64, 4], P('cell', 'net'), may hold values from 1 to 2, as said below
Outputs:
- updated: bfloat16 [32768, 256], P(('cell', 'net'))
- cell_grad: bfloat16 [32768, 256], P(('cell', 'net'))
- grad_in: float32 [256, 1024], replicated
- grad_net: float32 [256, 1024], replicated
- grad_bias: float32 [1024], replicated
- grad_out: float32 [1024, 256], replicated
Inputs may be any that keep to these rules, and one draw needn't show every extreme that they name: `block_count`: in each partition exactly one device of the net axis holds 2 live blocks; the others hold exactly 1.
All inputs are finite; a program needn't handle non-finite values.
Results may differ from a plain program's by a relative error of at most 0.0034.
Values may be sent and summed in bfloat16 or wider, within the bound.
A program may use at most 64 MiB of HBM per device.

v0:
```python
import math

import jax
import jax.numpy as jnp
from jax import lax
from jax.sharding import PartitionSpec as P

NETS_BLK = 128


def in_one_piece(arrays, axis, split_dim, concat_dim, along):
    widths = [a.shape[along] for a in arrays]
    both = jnp.concatenate(arrays, axis=along)
    whole = lax.all_to_all(both, axis, split_axis=split_dim, concat_axis=concat_dim, tiled=True)
    return tuple(jnp.split(whole, [sum(widths[:k]) for k in range(1, len(widths))], axis=along))


def sent_together(arrays, axis, dim, along):
    widths = [math.prod(a.shape[along:]) for a in arrays]
    both = jnp.concatenate(
        [a.reshape(*a.shape[:along], w) for a, w in zip(arrays, widths)], axis=along
    )
    whole = lax.all_gather(both, axis, axis=dim, tiled=True)
    pieces = jnp.split(whole, [sum(widths[:k]) for k in range(1, len(widths))], axis=along)
    return tuple(
        (b.reshape(*whole.shape[:along], *a.shape[along:]) for a, b in zip(arrays, pieces))
    )


def cut_along(x, dim, peers):
    before, after = (x.shape[:dim], x.shape[dim + 1 :])
    return jnp.moveaxis(x.reshape(*before, peers, -1, *after), dim, 0)


def summed_on_arrival(x, axis, dim):
    pieces = cut_along(x, dim, lax.axis_size(axis))
    arrived = lax.all_to_all(pieces, axis, split_axis=0, concat_axis=0, tiled=True)
    return arrived.sum(axis=0)


def side_by_side(arrays, axis, dim, along):
    widths = [a.shape[along] for a in arrays]
    both = jnp.concatenate(arrays, axis=along)
    whole = summed_on_arrival(both, axis, dim)
    return tuple(jnp.split(whole, [sum(widths[:k]) for k in range(1, len(widths))], axis=along))


def block_pass(table_x, table_g, net_ids, refs, w_in, w_net, bias, w_out):
    pin_feat = table_x[refs]
    pin_grad = table_g[refs]
    onehot = (net_ids[:, None] == jnp.arange(NETS_BLK, dtype=jnp.int32)[None, :]).astype(
        jnp.bfloat16
    )
    counts = jnp.sum(onehot.astype(jnp.float32), axis=0)
    inverse = 1.0 / jnp.maximum(counts, 1.0)
    net_sum = lax.dot_general(
        onehot, pin_feat, (((0,), (0,)), ((), ())), preferred_element_type=jnp.float32
    )
    net_feat = (net_sum * inverse[:, None]).astype(jnp.bfloat16)
    net_pre = jnp.dot(net_feat, w_net, preferred_element_type=jnp.float32).astype(jnp.bfloat16)
    pre_act = (
        jnp.dot(pin_feat, w_in, preferred_element_type=jnp.float32)
        + jnp.dot(onehot, net_pre, preferred_element_type=jnp.float32)
        + bias
    )
    hidden_full, gelu_back = jax.vjp(jax.nn.gelu, pre_act)
    hidden = hidden_full.astype(jnp.bfloat16)
    message = jnp.dot(hidden, w_out, preferred_element_type=jnp.float32)
    pulled = lax.dot_general(
        pin_grad, w_out, (((1,), (1,)), ((), ())), preferred_element_type=jnp.float32
    )
    pre_grad = gelu_back(pulled)[0].astype(jnp.bfloat16)
    grad_out = lax.dot_general(
        hidden, pin_grad, (((0,), (0,)), ((), ())), preferred_element_type=jnp.float32
    )
    grad_in = lax.dot_general(
        pin_feat, pre_grad, (((0,), (0,)), ((), ())), preferred_element_type=jnp.float32
    )
    grad_bias = jnp.sum(pre_grad.astype(jnp.float32), axis=0)
    net_grad = lax.dot_general(
        onehot, pre_grad, (((0,), (0,)), ((), ())), preferred_element_type=jnp.float32
    ).astype(jnp.bfloat16)
    grad_net = lax.dot_general(
        net_feat, net_grad, (((0,), (0,)), ((), ())), preferred_element_type=jnp.float32
    )
    feat_grad = (
        lax.dot_general(
            net_grad, w_net, (((1,), (1,)), ((), ())), preferred_element_type=jnp.float32
        )
        * inverse[:, None]
    ).astype(jnp.bfloat16)
    pin_back = lax.dot_general(
        pre_grad, w_in, (((1,), (1,)), ((), ())), preferred_element_type=jnp.float32
    ) + jnp.dot(onehot, feat_grad, preferred_element_type=jnp.float32)
    return (message, pin_back, (grad_in, grad_net, grad_bias, grad_out))


def local(cell_feat, out_grad, w_in, w_net, bias, w_out, send_idx, pin_net, pin_ref, block_count):
    part_count = lax.axis_size("cell")
    group_size = lax.axis_size("net")
    net_rank = lax.axis_index("net")
    local_rows = cell_feat.shape[0]
    feat_dim = cell_feat.shape[1]
    hidden_dim = w_in.shape[1]
    slot_count = send_idx.shape[2]
    chosen = send_idx[0]
    incoming_x, incoming_g = in_one_piece((cell_feat[chosen], out_grad[chosen]), "cell", 0, 0, 1)
    table_x = jnp.concatenate([cell_feat, incoming_x.reshape(-1, feat_dim)], axis=0)
    table_g = jnp.concatenate([out_grad, incoming_g.reshape(-1, feat_dim)], axis=0)
    table_len = table_x.shape[0]
    grads_zero = (
        jnp.zeros((feat_dim, hidden_dim), jnp.float32),
        jnp.zeros((feat_dim, hidden_dim), jnp.float32),
        jnp.zeros((hidden_dim,), jnp.float32),
        jnp.zeros((hidden_dim, feat_dim), jnp.float32),
    )
    initial = (
        jnp.zeros((table_len, feat_dim), jnp.float32),
        jnp.zeros((table_len, feat_dim), jnp.float32),
        grads_zero,
    )

    def accumulate(running, net_ids, refs):
        acc_y, acc_x, gradients = running
        message, pin_back, terms = block_pass(
            table_x, table_g, net_ids, refs, w_in, w_net, bias, w_out
        )
        return (
            acc_y.at[refs].add(message),
            acc_x.at[refs].add(pin_back),
            jax.tree.map(jnp.add, gradients, terms),
        )

    all_nets, all_refs, all_counts = sent_together((pin_net, pin_ref, block_count), "net", 1, 2)
    counts = all_counts[0]
    offsets = jnp.cumsum(counts) - counts
    live_total = jnp.sum(counts)
    turn_count = (live_total - net_rank + group_size - 1) // group_size

    def shared_block(turn_no, running):
        item_no = net_rank + group_size * turn_no
        owner_dev = jnp.sum((offsets <= item_no).astype(jnp.int32)) - 1
        slot_no = item_no - offsets[owner_dev]
        return accumulate(running, all_nets[0, owner_dev, slot_no], all_refs[0, owner_dev, slot_no])

    acc_y, acc_x, gradients = lax.fori_loop(0, turn_count, shared_block, initial)
    own_y = acc_y[:local_rows]
    own_x = acc_x[:local_rows]
    halo_y = acc_y[local_rows:].reshape(part_count, slot_count, feat_dim)
    halo_x = acc_x[local_rows:].reshape(part_count, slot_count, feat_dim)
    back_y, back_x = in_one_piece((halo_y, halo_x), "cell", 0, 0, 1)
    flat_targets = chosen.reshape(-1)
    own_y = own_y.at[flat_targets].add(back_y.reshape(-1, feat_dim))
    own_x = own_x.at[flat_targets].add(back_x.reshape(-1, feat_dim))
    summed_y, summed_x = side_by_side((own_y, own_x), "net", 0, 1)
    share_rows = local_rows // group_size
    base_feat = lax.dynamic_slice_in_dim(cell_feat, net_rank * share_rows, share_rows, 0)
    base_grad = lax.dynamic_slice_in_dim(out_grad, net_rank * share_rows, share_rows, 0)
    updated = (base_feat.astype(jnp.float32) + summed_y).astype(jnp.bfloat16)
    cell_grad = (base_grad.astype(jnp.float32) + summed_x).astype(jnp.bfloat16)
    grad_in, grad_net, grad_bias, grad_out = lax.psum(
        (gradients[0], gradients[1], gradients[2], gradients[3]), ("cell", "net")
    )
    return (updated, cell_grad, grad_in, grad_net, grad_bias, grad_out)


def solution(mesh):
    placed = (
        P("cell", None),
        P("cell", None),
        P(),
        P(),
        P(),
        P(),
        P("cell", None, None),
        P("cell", "net", None, None),
        P("cell", "net", None, None),
        P("cell", "net"),
    )
    return jax.shard_map(
        local,
        mesh=mesh,
        in_specs=placed,
        out_specs=(P(("cell", "net"), None), P(("cell", "net"), None), P(), P(), P(), P()),
        check_vma=False,
    )
```

profile of v0, /device:TPU:1, one launch (start us, length us, event | category | flops | bytes accessed | tf_op | source)
XLA Modules:
  0.0 454.3 jit_solution(16855415508506775089)
XLA Ops:
  7.2 0.7 compare_select_fusion.2
  8.1 4.5 gather_fusion.2
  12.6 3.9 gather_fusion.3
  16.5 1.1 pad_maximum_fusion.1
  17.7 13.6 %all-to-all-start = ((bf16[64,32,256]{2,1,0:T(8,128)(2,1)}), bf16[64,32,256]{2,1,0:T(8,128)(2,1)S(1)}, u32[]{:S(2)}, u32[]{:S(2)}) async-start(bf16[64,32,256]{2,1,0:T(8,128)(2,1)} %pad_maximum_fusion.1), calls=%async_computation | async-start | bytes 2097152 | tf_op jit(solution)/shard_map/all_to_all | solution.py:14
  32.0 7.8 %all_gather.3 = s32[1,4,2049]{2,0,1:T(1,128)S(1)} all-gather(s32[1,1,2049]{2,0,1:T(1,128)S(1)} %add_bitcast_fusion), channel_id=1, replica_groups=mesh['cell'=64,'net'=4] {'net'}, dimensions={1}, use_global_device_ids=true | all-gather | bytes 40980 | tf_op jit(solution)/shard_map/all_gather | solution.py:23
  39.8 0.7 slice_reduce_fusion.2
  41.5 15.9 %all-to-all-done = bf16[64,32,256]{2,1,0:T(8,128)(2,1)S(1)} async-done(((bf16[64,32,256]{2,1,0:T(8,128)(2,1)}), bf16[64,32,256]{2,1,0:T(8,128)(2,1)S(1)}, u32[]{:S(2)}, u32[]{:S(2)}) %all-to-all-start) | async-done | bytes 1048608 | tf_op jit(solution)/shard_map/all_to_all | solution.py:14
  57.5 1.2 pad_maximum_fusion.3
  59.0 1.1 broadcast.153
  60.0 1.1 broadcast.153.clone
  61.1 1.0 broadcast_in_dim.5
  62.2 48.2 %while.24 = (s32[]{:T(128)}, f32[1536,256]{1,0:T(8,128)S(1)}, f32[1536,256]{1,0:T(8,128)S(1)}, f32[256,1024]{1,0:T(8,128)}, f32[256,1024]{1,0:T(8,128)}, /*index...) while((s32[]{:T(128)}, f32[1536,256]{1,0:T(8,128)S(1)}, ...), condition=%wide.region_8.9_spmd, body=%wide.region_2.8_spmd.sunk | while | flops 2171603456 | bytes 63167552 | solution.py:146
  62.2 0.7 fusion.82
  64.3 0.7 dynamic_slice.44
  65.7 3.4 gather_fusion
  69.3 1.3 fusion.83
  70.6 3.0 fusion.84
  73.6 3.6 add_add_fusion.2
  77.3 3.4 gather_fusion.1
  80.7 3.5 convert_reduce_fusion.5
  84.2 1.0 copy-done
  85.2 1.2 convolution_convert_fusion.3
  86.4 2.6 fusion.86
  88.9 2.8 convolution_add_fusion.8
  91.7 4.4 scatter_fusion.1
  96.2 2.7 convolution_add_fusion.10
  98.9 0.5 convolution_add_fusion.9
  99.4 1.1 copy-done.6
  100.6 1.6 fusion.85
  102.2 4.4 scatter_fusion
  106.6 3.8 convolution_add_fusion.11
  110.5 1.5 pad_maximum_fusion
  112.0 8.3 %all-to-all-start.1 = ((f32[64,32,256]{2,1,0:T(8,128)}), f32[64,32,256]{2,1,0:T(8,128)}, u32[]{:S(2)}, u32[]{:S(2)}) async-start(f32[64,32,256]{2,1,0:T(8,128)} %pad_maximum_fusion), calls=%async_computation.1 | async-start | bytes 4194304 | tf_op jit(solution)/shard_map/all_to_all | solution.py:14
  120.6 0.5 all-reduce.3.cloned.1.call-update
  121.1 0.8 slice.12
  122.0 26.8 %all-to-all-done.1 = f32[64,32,256]{2,1,0:T(8,128)} async-done(((f32[64,32,256]{2,1,0:T(8,128)}), f32[64,32,256]{2,1,0:T(8,128)}, u32[]{:S(2)}, u32[]{:S(2)}) %all-to-all-start.1) | async-done | bytes 2097184 | tf_op jit(solution)/shard_map/all_to_all | solution.py:14
  148.8 1.7 fusion.21
  150.5 6.3 %scatter_fusion.2 = f32[512,256]{1,0:T(8,128)S(1)} fusion(f32[512,256]{1,0:T(8,128)S(1)} %copy-done.2, s32[1024]{0:T(1024)S(1)} %bitcast.104, f32[1024,256]{1,0:T(8,128)S(1)} %bitcast.89), kind=kCustom, calls=%fused_computation.6 | custom fusion | flops 262144 | bytes 3149824 | tf_op jit(solution)/shard_map/scatter-add | solution.py:153
  156.8 6.3 %scatter_fusion.3 = f32[512,256]{1,0:T(8,128)S(1)} fusion(f32[512,256]{1,0:T(8,128)S(1)} %slice.15, s32[1024]{0:T(1024)S(1)} %bitcast.105, f32[1024,256]{1,0:T(8,128)S(1)} %bitcast.88), kind=kCustom, calls=%fused_computation.7 | custom fusion | flops 262144 | bytes 3149824 | tf_op jit(solution)/shard_map/scatter-add | solution.py:154
  163.1 1.1 pad_maximum_fusion.2
  164.2 55.5 %all-to-all-start.2 = ((f32[4,128,512]{2,1,0:T(8,128)}), f32[4,128,512]{2,1,0:T(8,128)S(1)}, u32[]{:S(2)}, u32[]{:S(2)}) async-start(f32[4,128,512]{2,1,0:T(8,128)} %bitcast.17), calls=%async_computation.2 | async-start | bytes 2097152 | tf_op jit(solution)/shard_map/all_to_all | solution.py:37
  219.8 82.6 %psum.30 = f32[1024]{0:T(1024)} all-reduce(f32[1024]{0:T(1024)S(1)} %get-tuple-element.371), channel_id=1, replica_groups=mesh['cell'=64,'net'=4] {'cell','net'}, use_global_device_ids=true, to_apply=%region_14.15 | all-reduce | flops 1024 | bytes 8192 | tf_op jit(solution)/shard_map/psum | solution.py:161
  302.5 1.5 fusion.19
  304.0 139.0 %all-reduce.3.cloned.1.call-done = (f32[256,1024]{1,0:T(8,128)}, f32[256,1024]{1,0:T(8,128)}, f32[1024,256]{1,0:T(8,128)}) async-done(((f32[256,1024]{1,0:T(8,128)}, f32[256,1024]{1,0:T(8,128)}, f32[1024,256]{1,0:T(8,128)}), (f32[256,1024]{1,0:T(8,128)}, f32[256,1024]{1,0:T(8,128)}, f32[1024,256]{1,0:T(8,128)})) %all-reduce.3.cloned.1.call-update) | async-done | bytes 3145744 | tf_op jit(solution)/shard_map/psum | solution.py:161
  443.0 2.5 copy.67
  445.5 1.0 copy.68
  446.4 1.0 copy.69
  (60 shorter events, 1.6 us)
Async XLA Ops:
  8.0 4.5 copy-start.3
  16.5 14.8 %copy-start.13 = (s32[1,1,2,512]{3,2,1,0:T(2,128)S(1)}, s32[1,1,2,512]{3,2,1,0:T(2,128)}, u32[]{:S(2)}) copy-start(s32[1,1,2,512]{3,2,1,0:T(2,128)} %param.19) | copy-start | bytes 12292
  16.5 14.8 %copy-start.14 = (s32[1,1,2,512]{3,2,1,0:T(2,128)S(1)}, s32[1,1,2,512]{3,2,1,0:T(2,128)}, u32[]{:S(2)}) copy-start(s32[1,1,2,512]{3,2,1,0:T(2,128)} %param.20) | copy-start | bytes 12292
  17.7 39.8 %copy-start.4 = (bf16[512,256]{1,0:T(8,128)(2,1)S(1)}, bf16[512,256]{1,0:T(8,128)(2,1)}, u32[]{:S(2)}) copy-start(bf16[512,256]{1,0:T(8,128)(2,1)} %param.12) | copy-start | bytes 786436
  17.7 39.7 %all-to-all-start = ((bf16[64,32,256]{2,1,0:T(8,128)(2,1)}), bf16[64,32,256]{2,1,0:T(8,128)(2,1)S(1)}, u32[]{:S(2)}, u32[]{:S(2)}) async-start(bf16[64,32,256]{2,1,0:T(8,128)(2,1)} %pad_maximum_fusion.1), calls=%async_computation | async-start | bytes 2097152 | tf_op jit(solution)/shard_map/all_to_all | solution.py:14
  58.8 3.4 copy-start.11
  84.2 1.0 copy-start
  96.1 2.8 copy-start.1
  96.1 2.8 copy-start.5
  96.1 2.8 copy-start.7
  98.9 1.6 copy-start.6
  98.9 1.7 copy-start.15
  100.6 1.6 copy-start.8
  112.0 8.4 %copy-start.12 = (s32[1,64,16]{1,2,0:T(8,128)S(1)}, s32[1,64,16]{1,2,0:T(8,128)}, u32[]{:S(2)}) copy-start(s32[1,64,16]{1,2,0:T(8,128)} %param.18) | copy-start | bytes 12292
  112.0 36.8 %all-to-all-start.1 = ((f32[64,32,256]{2,1,0:T(8,128)}), f32[64,32,256]{2,1,0:T(8,128)}, u32[]{:S(2)}, u32[]{:S(2)}) async-start(f32[64,32,256]{2,1,0:T(8,128)} %pad_maximum_fusion), calls=%async_computation.1 | async-start | bytes 4194304 | tf_op jit(solution)/shard_map/all_to_all | solution.py:14
  120.3 322.7 %all-reduce.3.cloned.1.call-start = ((), (), s32[]{:S(2)}) async-start(), calls=%async_computation.3 | async-start | bytes 6291456 | tf_op jit(solution)/shard_map/psum | solution.py:161
  121.9 28.6 %copy-start.2 = (f32[512,256]{1,0:T(8,128)S(1)}, f32[512,256]{1,0:T(8,128)}, u32[]{:S(2)}) copy-start(f32[512,256]{1,0:T(8,128)} %slice.12) | copy-start | bytes 1572868
  164.2 138.1 %all-to-all-start.2 = ((f32[4,128,512]{2,1,0:T(8,128)}), f32[4,128,512]{2,1,0:T(8,128)S(1)}, u32[]{:S(2)}, u32[]{:S(2)}) async-start(f32[4,128,512]{2,1,0:T(8,128)} %bitcast.17), calls=%async_computation.2 | async-start | bytes 2097152 | tf_op jit(solution)/shard_map/all_to_all | solution.py:37
  443.0 2.5 copy-start.10
  443.0 3.4 copy-start.9
Sparse Core Ops, SparseCore 0:
  127.5 315.4 all-reduce.2
where the time goes:
time: 456 us; the launch traced here: 454 us
  waiting for transfers between devices  182 us (40%)
  blocking collectives  90.4 us (20%)
  starting transfers between devices  77.5 us (17%)
  other arithmetic  30.4 us (7%)
  local copies, waits for them, and re-layouts  29.3 us (6%)
  matrix products  26.6 us (6%)
  between operations  15.6 us (3%)
    psum x1, waiting for transfers between devices, local(): lax.psum((gradients[0], gradients[1], gradients[2], gradients[3]), ('cell...  139 us
    psum x1, blocking collectives, local(): lax.psum((gradients[0], gradients[1], gradients[2], gradients[3]), ('cell...  82.6 us
    all_to_all x1, starting transfers between devices, summed_on_arrival(): lax.all_to_all(pieces, axis, split_axis=0, concat_axis=0, tiled=True)  55.5 us
    all_to_all x2, waiting for transfers between devices, in_one_piece(): lax.all_to_all(both, axis, split_axis=split_dim, concat_axis=concat_dim,...  42.7 us
    all_to_all x2, starting transfers between devices, in_one_piece(): lax.all_to_all(both, axis, split_axis=split_dim, concat_axis=concat_dim,...  21.9 us
  transfers between devices with their start and end apart: 4, of which 3 were waited for; matrix products, arithmetic and copies ran while one was open for 4% of the time, Pallas kernels for 0%

commit v1 on v0

v1 whole, which is shorter than its diff:
```python
import functools

import jax
import jax.numpy as jnp
from jax import lax
from jax.experimental import pallas as pl
from jax.experimental.pallas import tpu as pltpu
from jax.sharding import PartitionSpec as P

MESH = pl.DeviceIdType.MESH
NETS = 128
F = 256
HB = 256
VM = pl.BlockSpec(memory_space=pltpu.VMEM)
BF = jnp.bfloat16
F32 = jnp.float32
Z_SIZE = 8


def dot(a, b, ca, cb):
    return lax.dot_general(a, b, (((ca,), (cb,)), ((), ())), preferred_element_type=F32)


def place():
    c = lax.axis_index("cell")
    n = lax.axis_index("net")
    core = lax.rem(n, 2)
    return c, n, core, n // 2, n + 1 - 2 * core, lax.rem(n + 2, 4)


def send(src, dst, sems, dev):
    copy = pltpu.make_async_remote_copy(
        src_ref=src, dst_ref=dst, send_sem=sems[0], recv_sem=sems[1], device_id=dev, device_id_type=MESH
    )
    copy.start()


def arrived(ref, sems, dev):
    pltpu.make_async_remote_copy(
        src_ref=ref, dst_ref=ref, send_sem=sems[0], recv_sem=sems[1], device_id=dev, device_id_type=MESH
    ).wait_recv()


def left(ref, sems, dev):
    pltpu.make_async_remote_copy(
        src_ref=ref, dst_ref=ref, send_sem=sems[0], recv_sem=sems[1], device_id=dev, device_id_type=MESH
    ).wait_send()


def hail(barrier, dev):
    pl.semaphore_signal(barrier, inc=1, device_id=dev, device_id_type=MESH)


def row_select(idx_row, rows):
    return (lax.broadcasted_iota(jnp.int32, (rows, idx_row.shape[1]), 0) == idx_row).astype(F32).astype(BF)


def halo_kernel(nc, slots, x_ref, g_ref, idx_ref, net_ref, ref_ref, cnt_ref, halo_ref, eid_ref,
                send_buf, ids_buf, ids_recv, send_sem, recv_sem):
    c, n, core, y_hi, mate, across = place()
    barrier = pltpu.get_barrier_semaphore()

    def greet(k, _):
        hail(barrier, (lax.rem(c + k, nc), n))
        return 0

    lax.fori_loop(1, nc, greet, 0)
    for m in range(1, 4):
        hail(barrier, (c, lax.rem(n + m, 4)))

    live = (cnt_ref[...] == 2).astype(jnp.int32)
    ids_buf[...] = jnp.zeros_like(ids_buf)
    ids_buf[0:1, :] = ref_ref[1:2, :] * live
    ids_buf[1:2, :] = net_ref[1:2, :] * live
    table = jnp.where(core == 0, x_ref[...].astype(F32), g_ref[...].astype(F32)).astype(BF)
    rows = x_ref.shape[0]
    send_buf[...] = dot(row_select(idx_ref[...], rows), table, 0, 0).astype(BF)
    mine = pl.ds(pl.multiple_of(c * slots, slots), slots)
    halo_ref[core, mine, :] = send_buf[mine, :]
    ids_recv[n] = ids_buf[...]

    pl.semaphore_wait(barrier, nc - 1 + 3)

    s_ids = (send_sem.at[0], recv_sem.at[0])
    s_a2a = (send_sem.at[1], recv_sem.at[1])
    s_mate = (send_sem.at[2], recv_sem.at[2])
    for m in range(1, 4):
        send(ids_buf, ids_recv.at[n], s_ids, (c, lax.rem(n + m, 4)))

    def push(k, _):
        d = lax.rem(c + k, nc)
        send(send_buf.at[pl.ds(pl.multiple_of(d * slots, slots), slots)], halo_ref.at[core, mine], s_a2a, (d, n))
        return 0

    lax.fori_loop(1, nc, push, 0)
    most = pl.ds(0, (nc - 1) * slots)
    arrived(halo_ref.at[core, most], s_a2a, (c, mate))
    send(halo_ref.at[core], halo_ref.at[core], s_mate, (c, mate))
    arrived(ids_recv.at[pl.ds(0, 3)], s_ids, (c, mate))
    eid_ref[...] = ids_recv[0] + ids_recv[1] + ids_recv[2] + ids_recv[3]
    arrived(halo_ref.at[core], s_mate, (c, mate))
    left(ids_recv.at[pl.ds(0, 3)], s_ids, (c, mate))
    left(halo_ref.at[core, most], s_a2a, (c, mate))
    left(halo_ref.at[core], s_mate, (c, mate))


def gelu_pair(x):
    k = 0.7978845608028654
    sq = x * x
    t = jnp.tanh(k * (x + 0.044715 * (sq * x)))
    half = 0.5 * (1.0 + t)
    slope = half + (0.5 * k) * x * (1.0 - t * t) * (1.0 + 3.0 * 0.044715 * sq)
    return x * half, slope


def block_kernel(x_ref, g_ref, halo_ref, net_ref, ref_ref, eid_ref, w_in_ref, w_net_ref, bias_ref, w_out_ref,
                 own_ref, back_ref, grad_ref, pin_x, pin_g, pin_xt, scat, into, onto, net_feat, net_feat_t, inv,
                 msg, pback, facc, bsum):
    n = lax.axis_index("net")
    cells = x_ref.shape[0]
    outer = halo_ref.shape[1]
    pins = ref_ref.shape[1]
    for b in range(2):
        refs = ref_ref[0:1, :] if b == 0 else eid_ref[0:1, :]
        nets = net_ref[0:1, :] if b == 0 else eid_ref[1:2, :]
        scat[b] = row_select(refs, cells + outer)
        near = scat[b, 0:cells, :]
        far = scat[b, cells:, :]
        px = (dot(near, x_ref[...], 0, 0) + dot(far, halo_ref[0], 0, 0)).astype(BF)
        pg = (dot(near, g_ref[...], 0, 0) + dot(far, halo_ref[1], 0, 0)).astype(BF)
        pin_x[b] = px
        pin_g[b] = pg
        pin_xt[b] = px.astype(F32).T.astype(BF)
        hit = (lax.broadcasted_iota(jnp.int32, (NETS, pins), 0) == nets).astype(F32)
        into[b] = hit.astype(BF)
        onto[b] = hit.T.astype(BF)
        inv_b = 1.0 / jnp.maximum(jnp.sum(hit, axis=1, keepdims=True), 1.0)
        inv[b] = jnp.broadcast_to(inv_b, (NETS, F))
        nf = dot(hit.astype(BF), px, 1, 0) * inv_b
        nf = nf.astype(BF)
        net_feat[b] = nf
        net_feat_t[b] = nf.astype(F32).T.astype(BF)
    msg[...] = jnp.zeros_like(msg)
    pback[...] = jnp.zeros_like(pback)
    facc[...] = jnp.zeros_like(facc)
    grad_ref[...] = jnp.zeros_like(grad_ref)
    bsum[...] = jnp.zeros_like(bsum)

    def item(i, _):
        b = i // 4
        hb = jnp.where(i < 4, i, n)
        cols = pl.ds(pl.multiple_of(hb * HB, HB), HB)
        w_in = w_in_ref[:, cols]
        w_net = w_net_ref[:, cols]
        w_out = w_out_ref[cols, :]
        px = pin_x[b]
        pg = pin_g[b]
        net_pre = dot(net_feat[b], w_net, 1, 0).astype(BF)
        pre_act = dot(px, w_in, 1, 0) + dot(onto[b], net_pre, 1, 0) + bias_ref[:, cols]
        act, slope = gelu_pair(pre_act)
        hidden = act.astype(BF)
        msg[b] += dot(hidden, w_out, 1, 0)
        pre_grad = (dot(pg, w_out, 1, 1) * slope).astype(BF)
        net_grad = dot(into[b], pre_grad, 1, 0).astype(BF)
        pback[b] += dot(pre_grad, w_in, 1, 1)
        facc[b] += dot(net_grad, w_net, 1, 1)
        g_in = dot(pin_xt[b], pre_grad, 1, 0)
        g_net = dot(net_feat_t[b], net_grad, 1, 0)
        g_out = dot(hidden, pg, 0, 0)
        for h in range(2):
            part = slice(h * 128, h * 128 + 128)
            grad_ref[h, hb] += g_in[:, part]
            grad_ref[h, 4 + hb] += g_net[:, part]
            grad_ref[h, 8 + hb] += g_out[:, part]
        bias_row = jnp.sum(pre_grad.astype(F32), axis=0, keepdims=True)
        mark = lax.broadcasted_iota(jnp.int32, (16, HB), 0) == hb
        bsum[...] += jnp.where(mark, bias_row, 0.0)
        return 0

    lax.fori_loop(0, 5, item, 0)
    for h in range(2):
        for k in range(16):
            grad_ref[h, 12, k * 16 : k * 16 + 16, :] = bsum[:, h * 128 : h * 128 + 128]
    for b in range(2):
        feat_grad = (facc[b] * inv[b]).astype(BF)
        pback[b] += dot(onto[b], feat_grad, 1, 0)
    for k, vals in enumerate((msg, pback)):
        for b in range(2):
            v = vals[b]
            high = v.astype(BF)
            low = (v - high.astype(F32)).astype(BF)
            near = dot(scat[b, 0:cells, :], high, 1, 0) + dot(scat[b, 0:cells, :], low, 1, 0)
            far = dot(scat[b, cells:, :], high, 1, 0) + dot(scat[b, cells:, :], low, 1, 0)
            if b == 0:
                own_ref[k] = near
                back_ref[k] = far
            else:
                own_ref[k] += near
                back_ref[k] += far


def return_kernel(nc, zs, slots, x_ref, g_ref, idx_ref, own_ref, back_ref, grad_ref, out_ref, gout_ref, bout_ref,
                  halo_in, own_in, grad_in, a2a_buf, a2a_in, half_buf, half_in, fin, g_send, g_recv, z_send, z_recv,
                  z_fin, z_all, g_fin, b_fin, send_sem, recv_sem):
    c, n, core, y_hi, mate, across = place()
    xy = nc // zs
    peers = 2 * xy
    gr = 256 // peers
    zr = 12 * gr // zs
    z = c // xy
    base = z * xy
    p = lax.rem(c, xy) * 2 + y_hi
    barrier = pltpu.get_barrier_semaphore()
    sem = lambda i: (send_sem.at[i], recv_sem.at[i])
    near = (c, mate)

    def greet(k, _):
        hail(barrier, (lax.rem(c + k, nc), n))
        return 0

    def greet_across(k, _):
        hail(barrier, (base + k, across))
        return 0

    lax.fori_loop(1, nc, greet, 0)
    lax.fori_loop(0, xy, greet_across, 0)
    hail(barrier, near)
    pl.semaphore_wait(barrier, nc - 1 + xy + 1)

    other = 1 - core
    send(back_ref.at[other], halo_in, sem(0), near)
    send(own_ref.at[other], own_in, sem(1), near)
    send(grad_ref.at[other], grad_in, sem(2), near)

    arrived(halo_in, sem(0), near)
    a2a_buf[...] = (back_ref[core] + halo_in[...]).astype(BF)
    mine = pl.ds(pl.multiple_of(c * slots, slots), slots)

    def push(k, _):
        d = lax.rem(c + k, nc)
        send(a2a_buf.at[pl.ds(pl.multiple_of(d * slots, slots), slots)], a2a_in.at[mine], sem(3), (d, n))
        return 0

    lax.fori_loop(1, nc, push, 0)
    a2a_in[mine, :] = a2a_buf[mine, :]

    arrived(grad_in, sem(2), near)
    g_send[...] = (grad_ref[core] + grad_in[...]).astype(BF)

    def push_xy(k, _):
        t = lax.rem(p + k, peers)
        rows = pl.ds(pl.multiple_of(t * gr, gr), gr)
        send(g_send.at[:, rows, :], g_recv.at[p], sem(4), (base + t // 2, lax.rem(t, 2) * 2 + core))
        return 0

    lax.fori_loop(1, peers, push_xy, 0)
    g_rows = pl.ds(pl.multiple_of(p * gr, gr), gr)
    g_recv[p] = g_send[:, g_rows, :]
    arrived(own_in, sem(1), near)
    half_all = own_ref[core] + own_in[...]

    arrived(g_recv.at[pl.ds(0, peers - 1)], sem(4), near)
    total = g_recv[0].astype(F32)
    for k in range(1, peers):
        total += g_recv[k].astype(F32)
    flat = total.reshape(13 * gr, 128)
    for k in range(zs):
        z_send[k, 0:zr, :] = flat[k * zr : k * zr + zr, :]
        z_send[k, zr : zr + 8, :] = flat[12 * gr : 12 * gr + 8, :]

    def push_z(k, _):
        t = lax.rem(z + k, zs)
        send(z_send.at[t], z_recv.at[z], sem(5), (t * xy + lax.rem(c, xy), n))
        return 0

    lax.fori_loop(1, zs, push_z, 0)
    z_recv[z] = z_send[z]

    most = pl.ds(0, (nc - 1) * slots)
    arrived(a2a_in.at[most], sem(3), near)
    rows = x_ref.shape[0]
    half_buf[...] = half_all + dot(row_select(idx_ref[...], rows), a2a_in[...], 1, 0)
    hr = rows // 2
    there = pl.ds(pl.multiple_of((1 - y_hi) * hr, hr), hr)
    here = pl.ds(pl.multiple_of(y_hi * hr, hr), hr)
    send(half_buf.at[there], half_in, sem(6), (c, across))

    arrived(z_recv.at[pl.ds(0, zs - 1)], sem(5), near)
    zsum = z_recv[0]
    for k in range(1, zs):
        zsum += z_recv[k]
    z_fin[...] = zsum[0:zr, :]
    b_fin[...] = zsum[zr : zr + 8, :]

    def push_zg(k, _):
        t = lax.rem(z + k, zs)
        send(z_fin, z_all.at[z], sem(7), (t * xy + lax.rem(c, xy), n))
        return 0

    lax.fori_loop(1, zs, push_zg, 0)
    z_all[z] = z_fin[...]
    bout_ref[core] = b_fin[...]
    send(b_fin, bout_ref.at[core], sem(8), near)

    arrived(half_in, sem(6), near)
    seed = jnp.where(core == 0, x_ref[here, :].astype(F32), g_ref[here, :].astype(F32))
    fin[...] = (half_buf[here, :] + half_in[...] + seed).astype(BF)
    qr = hr // 2
    theirs = pl.ds(pl.multiple_of((1 - core) * qr, qr), qr)
    ours = pl.ds(pl.multiple_of(core * qr, qr), qr)
    send(fin.at[theirs], out_ref.at[core], sem(9), near)
    out_ref[core] = fin[ours, :]

    arrived(z_all.at[pl.ds(0, zs - 1)], sem(7), near)
    g_fin[...] = z_all[...].reshape(12, gr, 128).astype(BF)

    def push_g(k, _):
        t = lax.rem(p + k, peers)
        send(g_fin, gout_ref.at[core, :, g_rows, :], sem(10), (base + t // 2, lax.rem(t, 2) * 2 + core))
        return 0

    lax.fori_loop(1, peers, push_g, 0)
    gout_ref[core, :, g_rows, :] = g_fin[...]
    arrived(g_recv.at[pl.ds(0, peers - 1), pl.ds(0, 12)], sem(10), near)
    send(gout_ref.at[core], gout_ref.at[core], sem(11), near)
    arrived(b_fin, sem(8), near)
    arrived(fin.at[ours], sem(9), near)
    arrived(gout_ref.at[core], sem(11), near)

    left(halo_in, sem(0), near)
    left(own_in, sem(1), near)
    left(grad_in, sem(2), near)
    left(a2a_in.at[most], sem(3), near)
    left(g_recv.at[pl.ds(0, peers - 1)], sem(4), near)
    left(z_recv.at[pl.ds(0, zs - 1)], sem(5), near)
    left(half_in, sem(6), near)
    left(z_all.at[pl.ds(0, zs - 1)], sem(7), near)
    left(b_fin, sem(8), near)
    left(fin.at[ours], sem(9), near)
    left(g_recv.at[pl.ds(0, peers - 1), pl.ds(0, 12)], sem(10), near)
    left(gout_ref.at[core], sem(11), near)


def shape(dims, kind):
    return jax.ShapeDtypeStruct(dims, kind)


def local(nc, zs, cell_feat, out_grad, w_in, w_net, bias, w_out, send_idx, pin_net, pin_ref, block_count):
    rows = cell_feat.shape[0]
    slots = send_idx.shape[2]
    outer = nc * slots
    pins = pin_ref.shape[3]
    hidden = w_in.shape[1]
    idx = send_idx.reshape(1, outer)
    nets = pin_net.reshape(2, pins)
    refs = pin_ref.reshape(2, pins)
    peers = 2 * nc // zs
    gr = 256 // peers
    zr = 12 * gr // zs
    dma = pltpu.SemaphoreType.DMA

    halo, eids = pl.pallas_call(
        functools.partial(halo_kernel, nc, slots),
        out_shape=(shape((2, outer, F), BF), shape((8, pins), jnp.int32)),
        in_specs=[VM] * 6,
        out_specs=(VM, VM),
        scratch_shapes=[
            pltpu.VMEM((outer, F), BF),
            pltpu.VMEM((8, pins), jnp.int32),
            pltpu.VMEM((4, 8, pins), jnp.int32),
            dma((3,)),
            dma((3,)),
        ],
        compiler_params=pltpu.CompilerParams(collective_id=0, has_side_effects=True),
        name="halo",
    )(cell_feat, out_grad, idx, nets, refs, block_count)

    own, back, grads = pl.pallas_call(
        block_kernel,
        out_shape=(shape((2, rows, F), F32), shape((2, outer, F), F32), shape((2, 13, 256, 128), F32)),
        in_specs=[VM] * 10,
        out_specs=(VM, VM, VM),
        scratch_shapes=[
            pltpu.VMEM((2, pins, F), BF),
            pltpu.VMEM((2, pins, F), BF),
            pltpu.VMEM((2, F, pins), BF),
            pltpu.VMEM((2, rows + outer, pins), BF),
            pltpu.VMEM((2, NETS, pins), BF),
            pltpu.VMEM((2, pins, NETS), BF),
            pltpu.VMEM((2, NETS, F), BF),
            pltpu.VMEM((2, F, NETS), BF),
            pltpu.VMEM((2, NETS, F), F32),
            pltpu.VMEM((2, pins, F), F32),
            pltpu.VMEM((2, pins, F), F32),
            pltpu.VMEM((2, NETS, F), F32),
            pltpu.VMEM((16, HB), F32),
        ],
        name="blocks",
    )(cell_feat, out_grad, halo, nets, refs, eids, w_in, w_net, bias.reshape(1, hidden), w_out)

    outs, gout, bout = pl.pallas_call(
        functools.partial(return_kernel, nc, zs, slots),
        out_shape=(shape((2, rows // 4, F), BF), shape((2, 12, 256, 128), BF), shape((2, 8, 128), F32)),
        in_specs=[VM] * 6,
        out_specs=(VM, VM, VM),
        scratch_shapes=[
            pltpu.VMEM((outer, F), F32),
            pltpu.VMEM((rows, F), F32),
            pltpu.VMEM((13, 256, 128), F32),
            pltpu.VMEM((outer, F), BF),
            pltpu.VMEM((outer, F), BF),
            pltpu.VMEM((rows, F), F32),
            pltpu.VMEM((rows // 2, F), F32),
            pltpu.VMEM((rows // 2, F), BF),
            pltpu.VMEM((13, 256, 128), BF),
            pltpu.VMEM((peers, 13, gr, 128), BF),
            pltpu.VMEM((zs, zr + 8, 128), F32),
            pltpu.VMEM((zs, zr + 8, 128), F32),
            pltpu.VMEM((zr, 128), F32),
            pltpu.VMEM((zs, zr, 128), F32),
            pltpu.VMEM((12, gr, 128), BF),
            pltpu.VMEM((8, 128), F32),
            dma((12,)),
            dma((12,)),
        ],
        compiler_params=pltpu.CompilerParams(collective_id=1, has_side_effects=True),
        name="back",
    )(cell_feat, out_grad, idx, own, back, grads)

    def whole(t):
        return gout[:, 4 * t : 4 * t + 4].transpose(2, 1, 0, 3).reshape(F, hidden).astype(F32)

    grad_out = gout[:, 8:12].transpose(1, 2, 0, 3).reshape(hidden, F).astype(F32)
    grad_bias = bout[:, 0:4].transpose(1, 0, 2).reshape(hidden)
    return (outs[0], outs[1], whole(0), whole(1), grad_bias, grad_out)


def solution(mesh):
    nc = mesh.shape["cell"]
    placed = (
        P("cell", None), P("cell", None), P(), P(), P(), P(),
        P("cell", None, None), P("cell", "net", None, None), P("cell", "net", None, None), P("cell", "net"),
    )
    return jax.shard_map(
        functools.partial(local, nc, Z_SIZE),
        mesh=mesh,
        in_specs=placed,
        out_specs=(P(("cell", "net"), None), P(("cell", "net"), None), P(), P(), P(), P()),
        check_vma=False,
    )
```

time: 456 us -> 118 us (0.26)
  waiting for transfers between devices: 182 us -> 0 us
  Pallas kernels: 0 us -> 105 us
  blocking collectives: 90.4 us -> 0 us
  starting transfers between devices: 77.5 us -> 0 us
  other arithmetic: 30.4 us -> 1.64 us
  matrix products: 26.6 us -> 0 us
  local copies, waits for them, and re-layouts: 29.3 us -> 9.41 us
  between operations: 15.6 us -> 1.33 us
    psum x1 -> x0, waiting for transfers between devices: 139 us -> none  [local(): lax.psum((gradients[0], gradients[1], gradients[2], gradients[3]), ('cell...]
    pallas_call x0 -> x3, Pallas kernels: none -> 105 us  [the longest x1 59 us: local(): pl.pallas_call(functools.partial(return_kernel, nc, zs, slots), out_shape...]
    psum x1 -> x0, blocking collectives: 82.6 us -> none  [local(): lax.psum((gradients[0], gradients[1], gradients[2], gradients[3]), ('cell...]
    all_to_all x3 -> x0, starting transfers between devices: 77.5 us -> none  [the longest x1 55.5 us: summed_on_arrival(): lax.all_to_all(pieces, axis, split_axis=0, concat_axis=0, tiled=True)]
    all_to_all x3 -> x0, waiting for transfers between devices: 42.7 us -> none  [the longest x2 42.7 us: in_one_piece(): lax.all_to_all(both, axis, split_axis=split_dim, concat_axis=concat_dim,...]
    dot_general x11 -> x0, matrix products: 26.6 us -> none  [the longest x1 3.79 us: block_pass(): lax.dot_general(hidden, pin_grad, (((0,), (0,)), ((), ())), preferred_ele...]
    scatter-add x4 -> x0, other arithmetic: 21.3 us -> none  [the longest x1 6.27 us: local(): own_y = own_y.at[flat_targets].add(back_y.reshape(-1, feat_dim))]
    gather x4 -> x0, local copies, waits for them, and re-layouts: 15.3 us -> none  [the longest x1 4.49 us: local(): cell_feat[chosen]]
  transfers between devices with their start and end apart: 4 -> 0, of which waited for: 3 -> 0; matrix products, arithmetic and copies ran while one was open for 4% -> 0% of each run, Pallas kernels for 0% -> 0%
where the time goes in v1:
time: 118 us
  Pallas kernels  105 us (89%)
  local copies, waits for them, and re-layouts  9.41 us (8%)
  other arithmetic  1.64 us (1%)
  between operations  1.33 us (1%)
    pallas_call x1, Pallas kernels, local(): pl.pallas_call(functools.partial(return_kernel, nc, zs, slots), out_shape...  59 us
    pallas_call x1, Pallas kernels, local(): pl.pallas_call(functools.partial(halo_kernel, nc, slots), out_shape=(shap...  28.9 us
    pallas_call x1, Pallas kernels, local(): pl.pallas_call(block_kernel, out_shape=(shape((2, rows, F), F32), shape((...  17.2 us
    unnamed x4, local copies, waits for them, and re-layouts  4.43 us

profile of v1, /device:TPU:1, one launch (start us, length us, event | category | flops | bytes accessed | tf_op | source)
XLA Modules:
  0.0 117.5 jit_solution(13941871817518551144)
XLA Ops:
  1.3 0.8 copy.17
  2.1 0.7 reshape.36.idx_ref
  2.7 28.9 %halo.1 = (bf16[2,1024,256]{2,1,0:T(8,128)(2,1)}, s32[8,512]{1,0:T(8,128)}) custom-call(bf16[512,256]{1,0:T(8,128)(2,1)} %x_ref.5, bf16[512,256]{1,0:T(8,128)(2,1)} %g_ref.5, s32[1,1024]{1,0:T(1,128)} %reshape.36.idx_ref, s32[2,512]{1,0:T(2,128)} %bitcast.27, s32[2,512]{1,0:T(2,128)} %bitcast.29, s32[1,1]{1,0:T(1,128)S(6)} %copy.27.cnt_ref), custom_call_target="tpu_custom_call" | custom-call | tf_op jit(solution)/shard_map/halo/pallas_call | solution.py:362
  31.6 17.2 %blocks.1 = (f32[2,512,256]{2,1,0:T(8,128)}, f32[2,1024,256]{2,1,0:T(8,128)}, f32[2,13,256,128]{3,2,1,0:T(8,128)}) custom-call(bf16[512,256]{1,0:T(8,128)(2,1)} %x_ref.5, bf16[512,256]{1,0:T(8,128)(2,1)} %g_ref.5, bf16[2,1024,256]{2,1,0:T(8,128)(2,1)} %get-tuple-element.14.halo_ref, s32[2,512]{1,0:T(2,128)} %bitcast.28, s32[2,512]{1,0:T(2,128)} %bitcast.30, ...), custom_call_target="tpu_custom_call" | custom-call | tf_op jit(solution)/shard_map/blocks/pallas_call | solution.py:378
  48.9 59.0 %back.1 = (bf16[2,128,256]{2,1,0:T(8,128)(2,1)}, bf16[2,12,256,128]{3,2,1,0:T(8,128)(2,1)}, f32[2,8,128]{2,1,0:T(8,128)}) custom-call(bf16[512,256]{1,0:T(8,128)(2,1)} %x_ref.5, bf16[512,256]{1,0:T(8,128)(2,1)} %g_ref.5, s32[1,1024]{1,0:T(1,128)} %reshape.36.idx_ref, f32[2,512,256]{2,1,0:T(8,128)} %get-tuple-element.16.own_ref, ...), custom_call_target="tpu_custom_call" | custom-call | tf_op jit(solution)/shard_map/back/pallas_call | solution.py:401
  107.9 1.5 %slice_bitcast_fusion = (bf16[128,256]{1,0:T(8,128)(2,1)}, bf16[128,256]{1,0:T(8,128)(2,1)}) fusion(bf16[2,128,256]{2,1,0:T(8,128)(2,1)} %get-tuple-element.19), kind=kLoop, calls=%fused_computation.4 | loop fusion | bytes 262144 | tf_op jit(solution)/shard_map/squeeze | solution.py:435
  109.4 0.7 slice_bitcast_fusion.2
  110.1 0.6 copy.20
  110.7 1.6 %convert_bitcast_fusion = (f32[4,256,2,128]{3,1,0,2:T(8,128)S(1)}, f32[256,4,2,128]{3,0,1,2:T(8,128)S(1)}, f32[256,4,2,128]{3,0,1,2:T(8,128)S(1)}) fusion(bf16[2,12,256,128]{3,2,1,0:T(8,128)(2,1)} %get-tuple-element.20), kind=kLoop, calls=%fused_computation.1 | loop fusion | flops 786432 | bytes 4718592 | tf_op jit(solution)/shard_map/convert_element_type | solution.py:433
  112.4 0.8 copy.21
  113.2 1.0 copy.26
  114.2 0.3 copy.19
  114.6 1.3 %copy.23 = f32[256,1024]{1,0:T(8,128)} copy(f32[256,1024]{0,1:T(8,128)S(1)} %bitcast.24) | data formatting | bytes 2097152
  115.9 0.3 copy.18
  116.2 1.3 %copy.22 = f32[256,1024]{1,0:T(8,128)} copy(f32[256,1024]{0,1:T(8,128)S(1)} %bitcast.25) | data formatting | bytes 2097152

commit v2 on v0

v2 whole, which is shorter than its diff:
```python
import functools

import jax
import jax.numpy as jnp
from jax import lax
from jax.experimental import pallas as pl
from jax.experimental.pallas import tpu as pltpu
from jax.sharding import PartitionSpec as P

MESH = pl.DeviceIdType.MESH
NETS = 128
F = 256
HB = 256
VM = pl.BlockSpec(memory_space=pltpu.VMEM)
ANY = pl.BlockSpec(memory_space=pl.ANY)
BF = jnp.bfloat16
F32 = jnp.float32
I32 = jnp.int32
Z_SIZE = 8


def dot(a, b, ca, cb):
    return lax.dot_general(a, b, (((ca,), (cb,)), ((), ())), preferred_element_type=F32)


def remote(src, dst, sems, dev):
    return pltpu.make_async_remote_copy(
        src_ref=src, dst_ref=dst, send_sem=sems[0], recv_sem=sems[1], device_id=dev, device_id_type=MESH
    )


def iota(dims, axis):
    return lax.broadcasted_iota(I32, dims, axis)


def ones_where(mask):
    return mask.astype(F32).astype(BF)


def gelu_pair(x):
    k = 0.7978845608028654
    sq = x * x
    t = jnp.tanh(k * (x + 0.044715 * (sq * x)))
    half = 0.5 * (1.0 + t)
    slope = half + (0.5 * k) * x * (1.0 - t * t) * (1.0 + 3.0 * 0.044715 * sq)
    return x * half, slope


def layer_kernel(nc, zs, slots,
                 x_ref, g_ref, idx_ref, net_ref, ref_ref, cnt_ref, w_in_hbm, w_net_hbm, bias_ref, w_out_hbm,
                 out_ref, gout_ref, bout_ref,
                 w_in_ref, w_net_ref, w_out_ref, send_buf, halo, ids_buf, ids_recv, sel_t, gath, scat, pin, pin_xt,
                 into, onto, net_feat, net_feat_t, inv, acc, facc, bsum, grads, grad_in, g_send, g_recv, b_in, b_send,
                 b_recv, far_buf, far_in, near_buf, near_in, a2a_buf, a2a_in, half_buf, half_in, fin,
                 z_send, z_recv, z_fin, z_all, g_fin, b_fin, w_sem, send_sem, recv_sem):
    c = lax.axis_index("cell")
    n = lax.axis_index("net")
    core = lax.rem(n, 2)
    other = 1 - core
    y_hi = n // 2
    mate = n + 1 - 2 * core
    across = lax.rem(n + 2, 4)
    xy = nc // zs
    peers = 2 * xy
    gr = 256 // peers
    zr = 12 * gr // zs
    z = c // xy
    base = z * xy
    p = lax.rem(c, xy) * 2 + y_hi
    near = (c, mate)
    cells = x_ref.shape[0]
    outer = nc * slots
    pins = ref_ref.shape[1]
    sem = lambda i: (send_sem.at[i], recv_sem.at[i])

    def send(src, dst, i, dev):
        remote(src, dst, sem(i), dev).start()

    def arrived(ref, i):
        remote(ref, ref, sem(i), near).wait_recv()

    def left(ref, i):
        remote(ref, ref, sem(i), near).wait_send()

    def xy_dev(t):
        return (base + t // 2, lax.rem(t, 2) * 2 + core)

    def rows_at(k, size):
        return pl.ds(pl.multiple_of(k * size, size), size)

    barrier = pltpu.get_barrier_semaphore()

    def hail(dev):
        pl.semaphore_signal(barrier, inc=1, device_id=dev, device_id_type=MESH)

    def greet(k, _):
        hail((lax.rem(c + k, nc), n))
        return 0

    def greet_across(k, _):
        hail((base + k, across))
        return 0

    lax.fori_loop(1, nc, greet, 0)
    lax.fori_loop(0, xy, greet_across, 0)
    hail(near)
    hail((c, 3 - n))

    loads = [
        pltpu.make_async_copy(src, dst, w_sem.at[i])
        for i, (src, dst) in enumerate(((w_in_hbm, w_in_ref), (w_net_hbm, w_net_ref), (w_out_hbm, w_out_ref)))
    ]
    for load in loads:
        load.start()

    idx = idx_ref[...]
    high = (idx // 2).astype(F32).astype(BF)
    low = lax.rem(idx, 2).astype(F32).astype(BF)
    pick = ones_where(iota((outer, nc), 0) // slots == iota((outer, nc), 1))
    spread = 2.0 * dot(pick, high, 1, 0) + dot(pick, low, 1, 0)
    keep = lax.rem(iota((outer, slots), 0), slots) == iota((outer, slots), 1)
    idx_col = jnp.sum(jnp.where(keep, spread, 0.0), axis=1, keepdims=True).astype(I32)
    table = jnp.where(core == 0, x_ref[...].astype(F32), g_ref[...].astype(F32)).astype(BF)
    send_buf[...] = dot(ones_where(iota((outer, cells), 1) == idx_col), table, 1, 0).astype(BF)
    live = (cnt_ref[...] == 2).astype(I32)
    ids_buf[...] = jnp.zeros_like(ids_buf)
    ids_buf[0:1, :] = ref_ref[1:2, :] * live
    ids_buf[1:2, :] = net_ref[1:2, :] * live

    pl.semaphore_wait(barrier, nc - 1 + xy + 2)

    mine = rows_at(c, slots)

    def push(k, _):
        d = lax.rem(c + k, nc)
        send(send_buf.at[rows_at(d, slots)], halo.at[core, mine], 0, (d, n))
        return 0

    lax.fori_loop(1, nc, push, 0)
    for m in range(1, 4):
        send(ids_buf, ids_recv.at[n], 1, (c, lax.rem(n + m, 4)))
    halo[core, mine, :] = send_buf[mine, :]
    ids_recv[n] = ids_buf[...]

    def lists(b, refs, nets):
        ids = jnp.concatenate([refs, nets, jnp.zeros((6, pins), I32)], axis=0).astype(F32)
        cols = ids.T.astype(I32)
        gath[b] = ones_where(iota((pins, cells + outer), 1) == cols[:, 0:1])
        scat[:, b * pins : (b + 1) * pins] = ones_where(iota((cells + outer, pins), 0) == refs)
        hit = (iota((NETS, pins), 0) == nets).astype(F32)
        into[b] = hit.astype(BF)
        onto[b] = ones_where(iota((pins, NETS), 1) == cols[:, 1:2])
        inv[b] = jnp.broadcast_to(1.0 / jnp.maximum(jnp.sum(hit, axis=1, keepdims=True), 1.0), (NETS, F))
        pin[0, b] = dot(gath[b, :, 0:cells], x_ref[...], 1, 0).astype(BF)
        pin[1, b] = dot(gath[b, :, 0:cells], g_ref[...], 1, 0).astype(BF)

    lists(0, ref_ref[0:1, :], net_ref[0:1, :])
    grads[...] = jnp.zeros_like(grads)
    acc[...] = jnp.zeros_like(acc)
    bsum[...] = jnp.zeros_like(bsum)
    facc[...] = jnp.zeros_like(facc)
    arrived(ids_recv.at[pl.ds(0, 3)], 1)
    ids = ids_recv[0] + ids_recv[1] + ids_recv[2] + ids_recv[3]
    lists(1, ids[0:1, :], ids[1:2, :])
    idx_row = jnp.broadcast_to(idx_col.astype(F32), (outer, 8)).T[0:1, :].astype(I32)
    sel_t[...] = ones_where(iota((cells, outer), 0) == idx_row)
    for load in loads:
        load.wait()

    most = pl.ds(0, (nc - 1) * slots)
    arrived(halo.at[core, most], 0)
    send(halo.at[core], halo.at[core], 2, near)

    def fetch(k):
        for b in range(2):
            pin[k, b] += dot(gath[b, :, cells:], halo[k], 1, 0).astype(BF)

    fetch(core)
    arrived(halo.at[core], 2)
    fetch(other)

    for b in range(2):
        px = pin[0, b]
        pin_xt[b] = px.astype(F32).T.astype(BF)
        nf = (dot(into[b], px, 1, 0) * inv[b]).astype(BF)
        net_feat[b] = nf
        net_feat_t[b] = nf.astype(F32).T.astype(BF)

    def item(b, hb):
        cols = rows_at(hb, HB)
        w_in = w_in_ref[:, cols]
        w_net = w_net_ref[:, cols]
        w_out = w_out_ref[cols, :]
        px = pin[0, b]
        pg = pin[1, b]
        net_pre = dot(net_feat[b], w_net, 1, 0).astype(BF)
        pre_act = dot(px, w_in, 1, 0) + dot(onto[b], net_pre, 1, 0) + bias_ref[:, cols]
        act, slope = gelu_pair(pre_act)
        hidden = act.astype(BF)
        acc[0, b] += dot(hidden, w_out, 1, 0)
        pre_grad = (dot(pg, w_out, 1, 1) * slope).astype(BF)
        net_grad = dot(into[b], pre_grad, 1, 0).astype(BF)
        acc[1, b] += dot(pre_grad, w_in, 1, 1)
        facc[b] += dot(net_grad, w_net, 1, 1)
        terms = (
            dot(pin_xt[b], pre_grad, 1, 0),
            dot(net_feat_t[b], net_grad, 1, 0),
            dot(hidden, pg, 0, 0),
        )
        for h in range(2):
            for t in range(3):
                grads[h, hb * 3 + t] += terms[t][:, h * 128 : h * 128 + 128]
        bias_row = jnp.sum(pre_grad.astype(F32), axis=0, keepdims=True)
        for h in range(2):
            bsum[h] += jnp.where(iota((16, 128), 0) == hb, bias_row[:, h * 128 : h * 128 + 128], 0.0)

    g_rows = rows_at(p, gr)

    def spread_grads(hb):
        part = pl.ds(hb * 3, 3)
        arrived(grad_in.at[part], 3 + hb)
        g_send[part] = (grads[core, part] + grad_in[part]).astype(BF)

        def push_xy(k, _):
            t = lax.rem(p + k, peers)
            send(g_send.at[part, rows_at(t, gr), :], g_recv.at[hb, p], 7 + hb, xy_dev(t))
            return 0

        lax.fori_loop(1, peers, push_xy, 0)
        g_recv[hb, p] = g_send[part, g_rows, :]

    item(1, n)

    def turn(hb, _):
        item(0, hb)
        part = pl.ds(hb * 3, 3)
        send(grads.at[other, part], grad_in.at[part], 3 + hb, near)

        @pl.when(hb > 0)
        def _():
            spread_grads(hb - 1)

        return 0

    lax.fori_loop(0, 4, turn, 0)
    send(bsum.at[other], b_in, 11, near)
    for b in range(2):
        feat_grad = (facc[b] * inv[b]).astype(BF)
        acc[1, b] += dot(onto[b], feat_grad, 1, 0)

    def scatter(k):
        vals = acc[k].reshape(2 * pins, F)
        high = vals.astype(BF)
        low = (vals - high.astype(F32)).astype(BF)
        out = scat[cells:, :]
        far_buf[k] = dot(out, high, 1, 0) + dot(out, low, 1, 0)
        out = scat[0:cells, :]
        near_buf[k] = dot(out, high, 1, 0) + dot(out, low, 1, 0)

    scatter(other)
    send(far_buf.at[other], far_in, 12, near)
    send(near_buf.at[other], near_in, 13, near)
    spread_grads(3)
    arrived(b_in, 11)
    b_send[...] = (bsum[core] + b_in[...]).astype(BF)

    def push_b(k, _):
        t = lax.rem(p + k, peers)
        send(b_send, b_recv.at[p], 14, xy_dev(t))
        return 0

    lax.fori_loop(1, peers, push_b, 0)
    b_recv[p] = b_send[...]
    scatter(core)
    arrived(far_in, 12)
    a2a_buf[...] = (far_buf[core] + far_in[...]).astype(BF)

    def push_back(k, _):
        d = lax.rem(c + k, nc)
        send(a2a_buf.at[rows_at(d, slots)], a2a_in.at[mine], 15, (d, n))
        return 0

    lax.fori_loop(1, nc, push_back, 0)
    a2a_in[mine, :] = a2a_buf[mine, :]

    arrived(near_in, 13)
    half_buf[...] = near_buf[core] + near_in[...]

    part_sums = []
    for hb in range(4):
        arrived(g_recv.at[hb, pl.ds(0, peers - 1)], 7 + hb)
        total = g_recv[hb, 0].astype(F32)
        for k in range(1, peers):
            total += g_recv[hb, k].astype(F32)
        part_sums.append(total.reshape(3 * gr, 128))
    flat = jnp.concatenate(part_sums, axis=0)
    arrived(b_recv.at[pl.ds(0, peers - 1)], 14)
    b_sum = b_recv[0].astype(F32)
    for k in range(1, peers):
        b_sum += b_recv[k].astype(F32)
    for k in range(zs):
        z_send[k, 0:zr, :] = flat[k * zr : k * zr + zr, :]
        z_send[k, zr : zr + 8, :] = b_sum[0:8, :]

    def z_dev(t):
        return (t * xy + lax.rem(c, xy), n)

    def push_z(k, _):
        t = lax.rem(z + k, zs)
        send(z_send.at[t], z_recv.at[z], 16, z_dev(t))
        return 0

    lax.fori_loop(1, zs, push_z, 0)
    z_recv[z] = z_send[z]
    arrived(z_recv.at[pl.ds(0, zs - 1)], 16)
    zsum = z_recv[0]
    for k in range(1, zs):
        zsum += z_recv[k]
    z_fin[...] = zsum[0:zr, :]
    b_fin[...] = zsum[zr : zr + 8, :]

    def push_zg(k, _):
        t = lax.rem(z + k, zs)
        send(z_fin, z_all.at[z], 17, z_dev(t))
        return 0

    lax.fori_loop(1, zs, push_zg, 0)
    z_all[z] = z_fin[...]
    bout_ref[core] = b_fin[...]
    send(b_fin, bout_ref.at[core], 18, near)

    arrived(a2a_in.at[most], 15)
    half_buf[...] += dot(sel_t[...], a2a_in[...], 1, 0)
    hr = cells // 2
    here = rows_at(y_hi, hr)
    send(half_buf.at[rows_at(1 - y_hi, hr)], half_in, 19, (c, across))

    arrived(z_all.at[pl.ds(0, zs - 1)], 17)
    g_fin[...] = z_all[...].reshape(12, gr, 128).astype(BF)

    def push_g(k, _):
        t = lax.rem(p + k, peers)
        send(g_fin, gout_ref.at[core, :, g_rows, :], 20, xy_dev(t))
        return 0

    lax.fori_loop(1, peers, push_g, 0)
    gout_ref[core, :, g_rows, :] = g_fin[...]

    arrived(half_in, 19)
    seed = jnp.where(core == 0, x_ref[here, :].astype(F32), g_ref[here, :].astype(F32))
    fin[...] = (half_buf[here, :] + half_in[...] + seed).astype(BF)
    qr = hr // 2
    ours = rows_at(core, qr)
    send(fin.at[rows_at(other, qr)], out_ref.at[core], 21, near)
    out_ref[core] = fin[ours, :]

    every = g_recv.at[pl.ds(0, 4), pl.ds(0, peers - 1)]
    arrived(every, 20)
    send(gout_ref.at[core], gout_ref.at[core], 22, near)
    arrived(b_fin, 18)
    arrived(fin.at[ours], 21)

    left(halo.at[core, most], 0)
    left(ids_recv.at[pl.ds(0, 3)], 1)
    left(halo.at[core], 2)
    for hb in range(4):
        left(grad_in.at[pl.ds(hb * 3, 3)], 3 + hb)
        left(g_recv.at[hb, pl.ds(0, peers - 1)], 7 + hb)
    left(b_in, 11)
    left(far_in, 12)
    left(near_in, 13)
    left(b_recv.at[pl.ds(0, peers - 1)], 14)
    left(a2a_in.at[most], 15)
    left(z_recv.at[pl.ds(0, zs - 1)], 16)
    left(z_all.at[pl.ds(0, zs - 1)], 17)
    left(b_fin, 18)
    left(half_in, 19)
    left(every, 20)
    left(fin.at[ours], 21)
    arrived(gout_ref.at[core], 22)
    left(gout_ref.at[core], 22)


def finish_kernel(outs_ref, gout_ref, bout_ref, y_ref, x_ref, gin_ref, gnet_ref, gbias_ref, gout_full):
    y_ref[...] = outs_ref[0]
    x_ref[...] = outs_ref[1]
    for hb in range(4):
        for h in range(2):
            cols = slice(hb * 256 + h * 128, hb * 256 + h * 128 + 128)
            gin_ref[:, cols] = gout_ref[h, hb * 3].astype(F32)
            gnet_ref[:, cols] = gout_ref[h, hb * 3 + 1].astype(F32)
            gout_full[hb * 256 : hb * 256 + 256, h * 128 : h * 128 + 128] = gout_ref[h, hb * 3 + 2].astype(F32)
            gbias_ref[:, cols] = bout_ref[h, hb : hb + 1, :]


def shape(dims, kind):
    return jax.ShapeDtypeStruct(dims, kind)


def local(nc, zs, cell_feat, out_grad, w_in, w_net, bias, w_out, send_idx, pin_net, pin_ref, block_count):
    rows = cell_feat.shape[0]
    slots = send_idx.shape[2]
    outer = nc * slots
    pins = pin_ref.shape[3]
    hidden = w_in.shape[1]
    peers = 2 * nc // zs
    gr = 256 // peers
    zr = 12 * gr // zs
    dma = pltpu.SemaphoreType.DMA
    vm = pltpu.VMEM

    outs, gout, bout = pl.pallas_call(
        functools.partial(layer_kernel, nc, zs, slots),
        out_shape=(shape((2, rows // 4, F), BF), shape((2, 12, 256, 128), BF), shape((2, 8, 128), F32)),
        in_specs=[VM] * 6 + [ANY, ANY, VM, ANY],
        out_specs=(VM, VM, VM),
        scratch_shapes=[
            vm((F, hidden), BF),
            vm((F, hidden), BF),
            vm((hidden, F), BF),
            vm((outer, F), BF),
            vm((2, outer, F), BF),
            vm((8, pins), I32),
            vm((4, 8, pins), I32),
            vm((rows, outer), BF),
            vm((2, pins, rows + outer), BF),
            vm((rows + outer, 2 * pins), BF),
            vm((2, 2, pins, F), BF),
            vm((2, F, pins), BF),
            vm((2, NETS, pins), BF),
            vm((2, pins, NETS), BF),
            vm((2, NETS, F), BF),
            vm((2, F, NETS), BF),
            vm((2, NETS, F), F32),
            vm((2, 2, pins, F), F32),
            vm((2, NETS, F), F32),
            vm((2, 16, 128), F32),
            vm((2, 12, 256, 128), F32),
            vm((12, 256, 128), F32),
            vm((12, 256, 128), BF),
            vm((4, peers, 3, gr, 128), BF),
            vm((16, 128), F32),
            vm((16, 128), BF),
            vm((peers, 16, 128), BF),
            vm((2, outer, F), F32),
            vm((outer, F), F32),
            vm((2, rows, F), F32),
            vm((rows, F), F32),
            vm((outer, F), BF),
            vm((outer, F), BF),
            vm((rows, F), F32),
            vm((rows // 2, F), F32),
            vm((rows // 2, F), BF),
            vm((zs, zr + 8, 128), F32),
            vm((zs, zr + 8, 128), F32),
            vm((zr, 128), F32),
            vm((zs, zr, 128), F32),
            vm((12, gr, 128), BF),
            vm((8, 128), F32),
            dma((3,)),
            dma((23,)),
            dma((23,)),
        ],
        compiler_params=pltpu.CompilerParams(collective_id=0, has_side_effects=True),
        name="layer",
    )(cell_feat, out_grad, send_idx.reshape(nc, slots), pin_net.reshape(2, pins), pin_ref.reshape(2, pins),
      block_count, w_in, w_net, bias.reshape(1, hidden), w_out)

    updated, cell_grad, grad_in, grad_net, grad_bias, grad_out = pl.pallas_call(
        finish_kernel,
        out_shape=(
            shape((rows // 4, F), BF), shape((rows // 4, F), BF), shape((F, hidden), F32),
            shape((F, hidden), F32), shape((1, hidden), F32), shape((hidden, F), F32),
        ),
        in_specs=[VM] * 3,
        out_specs=(VM,) * 6,
        name="finish",
    )(outs, gout, bout)
    return (updated, cell_grad, grad_in, grad_net, grad_bias.reshape(hidden), grad_out)


def solution(mesh):
    nc = mesh.shape["cell"]
    placed = (
        P("cell", None), P("cell", None), P(), P(), P(), P(),
        P("cell", None, None), P("cell", "net", None, None), P("cell", "net", None, None), P("cell", "net"),
    )
    return jax.shard_map(
        functools.partial(local, nc, Z_SIZE),
        mesh=mesh,
        in_specs=placed,
        out_specs=(P(("cell", "net"), None), P(("cell", "net"), None), P(), P(), P(), P()),
        check_vma=False,
    )
```

time: 456 us -> 88.6 us (0.19)
  waiting for transfers between devices: 182 us -> 0 us
  blocking collectives: 90.4 us -> 0 us
  Pallas kernels: 0 us -> 84.6 us
  starting transfers between devices: 77.5 us -> 0 us
  other arithmetic: 30.4 us -> 0 us
  local copies, waits for them, and re-layouts: 29.3 us -> 1.39 us
  matrix products: 26.6 us -> 0 us
  between operations: 15.6 us -> 1.29 us
    psum x1 -> x0, waiting for transfers between devices: 139 us -> none  [local(): lax.psum((gradients[0], gradients[1], gradients[2], gradients[3]), ('cell...]
    pallas_call x0 -> x2, Pallas kernels: none -> 84.6 us  [the longest x1 81.4 us: local(): pl.pallas_call(functools.partial(layer_kernel, nc, zs, slots), out_shape=...]
    psum x1 -> x0, blocking collectives: 82.6 us -> none  [local(): lax.psum((gradients[0], gradients[1], gradients[2], gradients[3]), ('cell...]
    all_to_all x3 -> x0, starting transfers between devices: 77.5 us -> none  [the longest x1 55.5 us: summed_on_arrival(): lax.all_to_all(pieces, axis, split_axis=0, concat_axis=0, tiled=True)]
    all_to_all x3 -> x0, waiting for transfers between devices: 42.7 us -> none  [the longest x2 42.7 us: in_one_piece(): lax.all_to_all(both, axis, split_axis=split_dim, concat_axis=concat_dim,...]
    dot_general x11 -> x0, matrix products: 26.6 us -> none  [the longest x1 3.79 us: block_pass(): lax.dot_general(hidden, pin_grad, (((0,), (0,)), ((), ())), preferred_ele...]
    scatter-add x4 -> x0, other arithmetic: 21.3 us -> none  [the longest x1 6.27 us: local(): own_y = own_y.at[flat_targets].add(back_y.reshape(-1, feat_dim))]
    gather x4 -> x0, local copies, waits for them, and re-layouts: 15.3 us -> none  [the longest x1 4.49 us: local(): cell_feat[chosen]]
  transfers between devices with their start and end apart: 4 -> 0, of which waited for: 3 -> 0; matrix products, arithmetic and copies ran while one was open for 4% -> 0% of each run, Pallas kernels for 0% -> 0%
where the time goes in v2:
time: 88.6 us; the launch traced here: 87.3 us
  Pallas kernels  84.6 us (95%)
  local copies, waits for them, and re-layouts  1.39 us (2%)
  between operations  1.29 us (1%)
    pallas_call x1, Pallas kernels, local(): pl.pallas_call(functools.partial(layer_kernel, nc, zs, slots), out_shape=...  81.4 us
    pallas_call x1, Pallas kernels, local(): pl.pallas_call(finish_kernel, out_shape=(shape((rows // 4, F), BF), shape...  3.21 us

profile of v2, /device:TPU:1, one launch (start us, length us, event | category | flops | bytes accessed | tf_op | source)
XLA Modules:
  0.0 87.3 jit_solution(4116427555469194771)
XLA Ops:
  1.3 1.4 %copy.16 = s32[1,64,16]{2,1,0:T(8,128)} copy(s32[1,64,16]{1,2,0:T(8,128)} %param.16) | data formatting | bytes 8192 | tf_op args[6]
  2.7 81.4 %layer.1 = (bf16[2,128,256]{2,1,0:T(8,128)(2,1)}, bf16[2,12,256,128]{3,2,1,0:T(8,128)(2,1)}, f32[2,8,128]{2,1,0:T(8,128)}) custom-call(bf16[512,256]{1,0:T(8,128)(2,1)} %x_ref.1, bf16[512,256]{1,0:T(8,128)(2,1)} %g_ref.1, s32[64,16]{1,0:T(8,128)} %bitcast.5, s32[2,512]{1,0:T(2,128)} %bitcast.6, s32[2,512]{1,0:T(2,128)} %bitcast.7, s32[1,1]{1,0:T(1,128)S(6)} %copy.17.cnt_ref, ...), custom_call_target="tpu_custom_call" | custom-call | tf_op jit(solution)/shard_map/layer/pallas_call | solution.py:412
  84.1 3.2 %finish.1 = (bf16[128,256]{1,0:T(8,128)(2,1)}, bf16[128,256]{1,0:T(8,128)(2,1)}, f32[256,1024]{1,0:T(8,128)}, f32[256,1024]{1,0:T(8,128)}, f32[1,1024]{1,0:T(1,128)}, /*index=5*/f32[1024,256]{1,0:T(8,128)}) custom-call(bf16[2,128,256]{2,1,0:T(8,128)(2,1)} %get-tuple-element.15.outs_ref, bf16[2,12,256,128]{3,2,1,0:T(8,128)(2,1)} %get-tuple-element.16.gout_ref, ...), custom_call_target="tpu_custom_call" | custom-call | tf_op jit(solution)/shard_map/finish/pallas_call | solution.py:469

commit v3 on v2

--- a/solution.py
+++ b/solution.py
@@ -13,10 +13,12 @@
 HB = 256
 VM = pl.BlockSpec(memory_space=pltpu.VMEM)
 ANY = pl.BlockSpec(memory_space=pl.ANY)
+HBM = pl.BlockSpec(memory_space=pltpu.HBM)
 BF = jnp.bfloat16
 F32 = jnp.float32
 I32 = jnp.int32
 Z_SIZE = 8
+WAVES = (2, 2)
 
 
 def dot(a, b, ca, cb):
@@ -39,20 +41,20 @@
 
 def gelu_pair(x):
     k = 0.7978845608028654
+    q = k * 0.044715
     sq = x * x
-    t = jnp.tanh(k * (x + 0.044715 * (sq * x)))
-    half = 0.5 * (1.0 + t)
-    slope = half + (0.5 * k) * x * (1.0 - t * t) * (1.0 + 3.0 * 0.044715 * sq)
-    return x * half, slope
+    half = 0.5 + 0.5 * jnp.tanh(x * (k + q * sq))
+    act = x * half
+    return act, half + (act - act * half) * (2.0 * k + 6.0 * q * sq)
 
 
 def layer_kernel(nc, zs, slots,
                  x_ref, g_ref, idx_ref, net_ref, ref_ref, cnt_ref, w_in_hbm, w_net_hbm, bias_ref, w_out_hbm,
-                 out_ref, gout_ref, bout_ref,
+                 out_ref, gout_ref, gz_ref, bout_ref,
                  w_in_ref, w_net_ref, w_out_ref, send_buf, halo, ids_buf, ids_recv, sel_t, gath, scat, pin, pin_xt,
-                 into, onto, net_feat, net_feat_t, inv, acc, facc, bsum, grads, grad_in, g_send, g_recv, b_in, b_send,
-                 b_recv, far_buf, far_in, near_buf, near_in, a2a_buf, a2a_in, half_buf, half_in, fin,
-                 z_send, z_recv, z_fin, z_all, g_fin, b_fin, w_sem, send_sem, recv_sem):
+                 into, onto, net_feat, net_feat_t, inv, hid, slope_g, net_g, vals, bsum, grads, grad_in, g_send, g_recv,
+                 b_in, b_send, b_recv, far_buf, far_in, near_buf, near_in, a2a_buf, a2a_in, half_buf, half_in, fin,
+                 z_send, z_recv, z_fin, z_all, g_fin, b_fin, q_recv, r_send, r_recv, gz_fin, w_sem, send_sem, recv_sem):
     c = lax.axis_index("cell")
     n = lax.axis_index("net")
     core = lax.rem(n, 2)
@@ -63,7 +65,9 @@
     xy = nc // zs
     peers = 2 * xy
     gr = 256 // peers
-    zr = 12 * gr // zs
+    zr = 8 * gr // zs
+    zq = 256 // zs
+    zz = 4 * zq // peers
     z = c // xy
     base = z * xy
     p = lax.rem(c, xy) * 2 + y_hi
@@ -85,6 +89,9 @@
     def xy_dev(t):
         return (base + t // 2, lax.rem(t, 2) * 2 + core)
 
+    def z_dev(t):
+        return (t * xy + lax.rem(c, xy), n)
+
     def rows_at(k, size):
         return pl.ds(pl.multiple_of(k * size, size), size)
 
@@ -117,7 +124,7 @@
     high = (idx // 2).astype(F32).astype(BF)
     low = lax.rem(idx, 2).astype(F32).astype(BF)
     pick = ones_where(iota((outer, nc), 0) // slots == iota((outer, nc), 1))
-    spread = 2.0 * dot(pick, high, 1, 0) + dot(pick, low, 1, 0)
+    spread = 2.0 * dot(pick, high, 1, 1) + dot(pick, low, 1, 1)
     keep = lax.rem(iota((outer, slots), 0), slots) == iota((outer, slots), 1)
     idx_col = jnp.sum(jnp.where(keep, spread, 0.0), axis=1, keepdims=True).astype(I32)
     table = jnp.where(core == 0, x_ref[...].astype(F32), g_ref[...].astype(F32)).astype(BF)
@@ -156,9 +163,7 @@
 
     lists(0, ref_ref[0:1, :], net_ref[0:1, :])
     grads[...] = jnp.zeros_like(grads)
-    acc[...] = jnp.zeros_like(acc)
     bsum[...] = jnp.zeros_like(bsum)
-    facc[...] = jnp.zeros_like(facc)
     arrived(ids_recv.at[pl.ds(0, 3)], 1)
     ids = ids_recv[0] + ids_recv[1] + ids_recv[2] + ids_recv[3]
     lists(1, ids[0:1, :], ids[1:2, :])
@@ -186,8 +191,9 @@
         net_feat[b] = nf
         net_feat_t[b] = nf.astype(F32).T.astype(BF)
 
-    def item(b, hb):
+    def item(b, hb, slot):
         cols = rows_at(hb, HB)
+        place = rows_at(slot, HB)
         w_in = w_in_ref[:, cols]
         w_net = w_net_ref[:, cols]
         w_out = w_out_ref[cols, :]
@@ -197,15 +203,15 @@
         pre_act = dot(px, w_in, 1, 0) + dot(onto[b], net_pre, 1, 0) + bias_ref[:, cols]
         act, slope = gelu_pair(pre_act)
         hidden = act.astype(BF)
-        acc[0, b] += dot(hidden, w_out, 1, 0)
+        hid[:, place] = hidden
         pre_grad = (dot(pg, w_out, 1, 1) * slope).astype(BF)
         net_grad = dot(into[b], pre_grad, 1, 0).astype(BF)
-        acc[1, b] += dot(pre_grad, w_in, 1, 1)
-        facc[b] += dot(net_grad, w_net, 1, 1)
+        slope_g[:, place] = pre_grad
+        net_g[:, place] = net_grad
         terms = (
             dot(pin_xt[b], pre_grad, 1, 0),
+            dot(hidden, pg, 0, 0),
             dot(net_feat_t[b], net_grad, 1, 0),
-            dot(hidden, pg, 0, 0),
         )
         for h in range(2):
             for t in range(3):
@@ -221,18 +227,27 @@
         arrived(grad_in.at[part], 3 + hb)
         g_send[part] = (grads[core, part] + grad_in[part]).astype(BF)
 
+        pair = pl.ds(hb * 3, 2)
+
         def push_xy(k, _):
             t = lax.rem(p + k, peers)
-            send(g_send.at[part, rows_at(t, gr), :], g_recv.at[hb, p], 7 + hb, xy_dev(t))
+            send(g_send.at[pair, rows_at(t, gr), :], g_recv.at[hb, p], 7 + hb, xy_dev(t))
             return 0
 
+        def push_q(k, _):
+            t = lax.rem(z + k, zs)
+            send(g_send.at[hb * 3 + 2, rows_at(t, zq), :], q_recv.at[hb, z], 25 + hb, z_dev(t))
+            return 0
+
         lax.fori_loop(1, peers, push_xy, 0)
-        g_recv[hb, p] = g_send[part, g_rows, :]
-
-    item(1, n)
+        lax.fori_loop(1, zs, push_q, 0)
+        g_recv[hb, p] = g_send[pair, g_rows, :]
+        q_recv[hb, z] = g_send[hb * 3 + 2, rows_at(z, zq), :]
+
+    item(1, n, 4)
 
     def turn(hb, _):
-        item(0, hb)
+        item(0, hb, hb)
         part = pl.ds(hb * 3, 3)
         send(grads.at[other, part], grad_in.at[part], 3 + hb, near)
 
@@ -244,23 +259,27 @@
 
     lax.fori_loop(0, 4, turn, 0)
     send(bsum.at[other], b_in, 11, near)
-    for b in range(2):
-        feat_grad = (facc[b] * inv[b]).astype(BF)
-        acc[1, b] += dot(onto[b], feat_grad, 1, 0)
+    wide = 4 * HB
+    extra = rows_at(n, HB)
+    pairs = (
+        (slice(0, wide), w_in_ref[...], w_net_ref[...], w_out_ref[...]),
+        (slice(wide, wide + HB), w_in_ref[:, extra], w_net_ref[:, extra], w_out_ref[extra, :]),
+    )
+    backs = []
+    for b, (cols, w_in, w_net, w_out) in enumerate(pairs):
+        mine_b = slice(b * pins, (b + 1) * pins)
+        vals[0, mine_b, :] = dot(hid[:, cols], w_out, 1, 0).astype(BF)
+        feat_grad = (dot(net_g[:, cols], w_net, 1, 1) * inv[b]).astype(BF)
+        vals[1, mine_b, :] = (dot(slope_g[:, cols], w_in, 1, 1) + dot(onto[b], feat_grad, 1, 0)).astype(BF)
+    spread_grads(3)
 
     def scatter(k):
-        vals = acc[k].reshape(2 * pins, F)
-        high = vals.astype(BF)
-        low = (vals - high.astype(F32)).astype(BF)
-        out = scat[cells:, :]
-        far_buf[k] = dot(out, high, 1, 0) + dot(out, low, 1, 0)
-        out = scat[0:cells, :]
-        near_buf[k] = dot(out, high, 1, 0) + dot(out, low, 1, 0)
+        far_buf[k] = dot(scat[cells:, :], vals[k], 1, 0)
+        near_buf[k] = dot(scat[0:cells, :], vals[k], 1, 0)
 
     scatter(other)
     send(far_buf.at[other], far_in, 12, near)
     send(near_buf.at[other], near_in, 13, near)
-    spread_grads(3)
     arrived(b_in, 11)
     b_send[...] = (bsum[core] + b_in[...]).astype(BF)
 
@@ -272,6 +291,7 @@
     lax.fori_loop(1, peers, push_b, 0)
     b_recv[p] = b_send[...]
     scatter(core)
+
     arrived(far_in, 12)
     a2a_buf[...] = (far_buf[core] + far_in[...]).astype(BF)
 
@@ -280,9 +300,10 @@
         send(a2a_buf.at[rows_at(d, slots)], a2a_in.at[mine], 15, (d, n))
         return 0
 
-    lax.fori_loop(1, nc, push_back, 0)
+    first = 1 + (nc - 1) * WAVES[0] // 8
+    second = first + (nc - 1) * WAVES[1] // 8
+    lax.fori_loop(1, first, push_back, 0)
     a2a_in[mine, :] = a2a_buf[mine, :]
-
     arrived(near_in, 13)
     half_buf[...] = near_buf[core] + near_in[...]
 
@@ -292,7 +313,7 @@
         total = g_recv[hb, 0].astype(F32)
         for k in range(1, peers):
             total += g_recv[hb, k].astype(F32)
-        part_sums.append(total.reshape(3 * gr, 128))
+        part_sums.append(total.reshape(2 * gr, 128))
     flat = jnp.concatenate(part_sums, axis=0)
     arrived(b_recv.at[pl.ds(0, peers - 1)], 14)
     b_sum = b_recv[0].astype(F32)
@@ -302,22 +323,44 @@
         z_send[k, 0:zr, :] = flat[k * zr : k * zr + zr, :]
         z_send[k, zr : zr + 8, :] = b_sum[0:8, :]
 
-    def z_dev(t):
-        return (t * xy + lax.rem(c, xy), n)
-
     def push_z(k, _):
         t = lax.rem(z + k, zs)
         send(z_send.at[t], z_recv.at[z], 16, z_dev(t))
         return 0
 
     lax.fori_loop(1, zs, push_z, 0)
+
+    lax.fori_loop(first, second, push_back, 0)
     z_recv[z] = z_send[z]
+
+    q_sums = []
+    for hb in range(4):
+        arrived(q_recv.at[hb, pl.ds(0, zs - 1)], 25 + hb)
+        total = q_recv[hb, 0].astype(F32)
+        for k in range(1, zs):
+            total += q_recv[hb, k].astype(F32)
+        q_sums.append(total)
+    r_send[...] = jnp.concatenate(q_sums, axis=0).reshape(peers, zz, 128)
+
+    def push_r(k, _):
+        t = lax.rem(p + k, peers)
+        send(r_send.at[t], r_recv.at[p], 29, xy_dev(t))
+        return 0
+
+    lax.fori_loop(1, peers, push_r, 0)
+    r_recv[p] = r_send[p]
+
     arrived(z_recv.at[pl.ds(0, zs - 1)], 16)
     zsum = z_recv[0]
     for k in range(1, zs):
         zsum += z_recv[k]
-    z_fin[...] = zsum[0:zr, :]
+    z_fin[0:zr, :] = zsum[0:zr, :]
     b_fin[...] = zsum[zr : zr + 8, :]
+    arrived(r_recv.at[pl.ds(0, peers - 1)], 29)
+    rsum = r_recv[0]
+    for k in range(1, peers):
+        rsum += r_recv[k]
+    z_fin[zr : zr + zz, :] = rsum
 
     def push_zg(k, _):
         t = lax.rem(z + k, zs)
@@ -325,40 +368,64 @@
         return 0
 
     lax.fori_loop(1, zs, push_zg, 0)
+    lax.fori_loop(second, nc, push_back, 0)
     z_all[z] = z_fin[...]
     bout_ref[core] = b_fin[...]
     send(b_fin, bout_ref.at[core], 18, near)
 
+    arrived(z_all.at[pl.ds(0, zs - 1)], 17)
+    g_fin[...] = z_all[:, 0:zr, :].reshape(8, gr, 128).astype(BF)
+    gz_fin[...] = z_all[:, zr : zr + zz, :].reshape(zs * zz, 128).astype(BF)
+    xn = peers // 4
+    x_at = p // 4
+    y_at = lax.rem(p, 4)
+    one, two = pl.ds(0, 6), pl.ds(6, 2)
+
+    def to_x(k):
+        return xy_dev(lax.rem(x_at + k, xn) * 4 + y_at)
+
+    def to_y(k):
+        return xy_dev(x_at * 4 + lax.rem(y_at + k, 4))
+
+    for k in range(1, xn):
+        send(g_fin.at[one], gout_ref.at[core, one, x_at, y_at], 20, to_x(k))
+    for k in range(1, 4):
+        send(g_fin.at[two], gout_ref.at[core, two, x_at, y_at], 22, to_y(k))
+        send(gz_fin, gz_ref.at[core, x_at, y_at], 30, to_y(k))
+    gout_ref[core, :, x_at, y_at] = g_fin[...]
+    gz_ref[core, x_at, y_at] = gz_fin[...]
+    if xn > 1:
+        arrived(gout_ref.at[core, one, pl.ds(0, xn - 1), 0], 20)
+    for k in range(1, 4):
+        send(gout_ref.at[core, one, :, y_at], gout_ref.at[core, one, :, y_at], 21, to_y(k))
+    arrived(gout_ref.at[core, two, 0, pl.ds(0, 3)], 22)
+    arrived(gz_ref.at[core, 0, pl.ds(0, 3)], 30)
+    for k in range(1, xn):
+        send(gout_ref.at[core, two, x_at], gout_ref.at[core, two, x_at], 23, to_x(k))
+        send(gz_ref.at[core, x_at], gz_ref.at[core, x_at], 31, to_x(k))
+
     arrived(a2a_in.at[most], 15)
     half_buf[...] += dot(sel_t[...], a2a_in[...], 1, 0)
-    hr = cells // 2
-    here = rows_at(y_hi, hr)
-    send(half_buf.at[rows_at(1 - y_hi, hr)], half_in, 19, (c, across))
-
-    arrived(z_all.at[pl.ds(0, zs - 1)], 17)
-    g_fin[...] = z_all[...].reshape(12, gr, 128).astype(BF)
-
-    def push_g(k, _):
-        t = lax.rem(p + k, peers)
-        send(g_fin, gout_ref.at[core, :, g_rows, :], 20, xy_dev(t))
-        return 0
-
-    lax.fori_loop(1, peers, push_g, 0)
-    gout_ref[core, :, g_rows, :] = g_fin[...]
-
+    fin[...] = half_buf[...].astype(BF)
+    qr = cells // 4
+    ours = rows_at(n, qr)
+    for k, q in enumerate((mate, across, 3 - n)):
+        send(fin.at[rows_at(q, qr)], half_in.at[k], 19, (c, q))
     arrived(half_in, 19)
-    seed = jnp.where(core == 0, x_ref[here, :].astype(F32), g_ref[here, :].astype(F32))
-    fin[...] = (half_buf[here, :] + half_in[...] + seed).astype(BF)
-    qr = hr // 2
-    ours = rows_at(core, qr)
-    send(fin.at[rows_at(other, qr)], out_ref.at[core], 21, near)
-    out_ref[core] = fin[ours, :]
-
-    every = g_recv.at[pl.ds(0, 4), pl.ds(0, peers - 1)]
-    arrived(every, 20)
-    send(gout_ref.at[core], gout_ref.at[core], 22, near)
+    kept = half_buf[ours, :] + half_in[1].astype(F32)
+    swapped = half_in[0].astype(F32) + half_in[2].astype(F32)
+    as_x = jnp.where(core == 0, kept, swapped)
+    as_g = jnp.where(core == 0, swapped, kept)
+    out_ref[0] = (as_x + x_ref[ours, :].astype(F32)).astype(BF)
+    out_ref[1] = (as_g + g_ref[ours, :].astype(F32)).astype(BF)
+
+    arrived(gout_ref.at[core, one, :, pl.ds(0, 3)], 21)
+    if xn > 1:
+        arrived(gout_ref.at[core, two, pl.ds(0, xn - 1)], 23)
+        arrived(gz_ref.at[core, pl.ds(0, xn - 1)], 31)
+    send(gout_ref.at[core], gout_ref.at[core], 24, near)
+    send(gz_ref.at[core], gz_ref.at[core], 32, near)
     arrived(b_fin, 18)
-    arrived(fin.at[ours], 21)
 
     left(halo.at[core, most], 0)
     left(ids_recv.at[pl.ds(0, 3)], 1)
@@ -366,6 +433,7 @@
     for hb in range(4):
         left(grad_in.at[pl.ds(hb * 3, 3)], 3 + hb)
         left(g_recv.at[hb, pl.ds(0, peers - 1)], 7 + hb)
+        left(q_recv.at[hb, pl.ds(0, zs - 1)], 25 + hb)
     left(b_in, 11)
     left(far_in, 12)
     left(near_in, 13)
@@ -374,23 +442,52 @@
     left(z_recv.at[pl.ds(0, zs - 1)], 16)
     left(z_all.at[pl.ds(0, zs - 1)], 17)
     left(b_fin, 18)
+    left(r_recv.at[pl.ds(0, peers - 1)], 29)
+    left(gz_ref.at[core, 0, pl.ds(0, 3)], 30)
     left(half_in, 19)
-    left(every, 20)
-    left(fin.at[ours], 21)
-    arrived(gout_ref.at[core], 22)
-    left(gout_ref.at[core], 22)
-
-
-def finish_kernel(outs_ref, gout_ref, bout_ref, y_ref, x_ref, gin_ref, gnet_ref, gbias_ref, gout_full):
-    y_ref[...] = outs_ref[0]
-    x_ref[...] = outs_ref[1]
+    left(gout_ref.at[core, one, :, pl.ds(0, 3)], 21)
+    left(gout_ref.at[core, two, 0, pl.ds(0, 3)], 22)
+    if xn > 1:
+        left(gout_ref.at[core, one, pl.ds(0, xn - 1), 0], 20)
+        left(gout_ref.at[core, two, pl.ds(0, xn - 1)], 23)
+        left(gz_ref.at[core, pl.ds(0, xn - 1)], 31)
+    arrived(gout_ref.at[core], 24)
+    left(gout_ref.at[core], 24)
+    arrived(gz_ref.at[core], 32)
+    left(gz_ref.at[core], 32)
+
+
+def finish_kernel(zs, outs_ref, gout_ref, gz_ref, bout_ref, y_ref, x_ref, gin_ref, gnet_ref, gbias_ref, gout_full,
+                  gin, gnet, gfull, gbias, sem):
+    copies = []
+    zq = 256 // zs
+    zz = gz_ref.shape[2] // zs
+    per = gz_ref.shape[1] // 4
+
+    def put(src, dst):
+        copies.append(pltpu.make_async_copy(src, dst, sem.at[len(copies)]))
+        copies[-1].start()
+
+    put(outs_ref.at[0], y_ref)
+    put(outs_ref.at[1], x_ref)
     for hb in range(4):
+        block = slice(hb * 256, hb * 256 + 256)
         for h in range(2):
             cols = slice(hb * 256 + h * 128, hb * 256 + h * 128 + 128)
-            gin_ref[:, cols] = gout_ref[h, hb * 3].astype(F32)
-            gnet_ref[:, cols] = gout_ref[h, hb * 3 + 1].astype(F32)
-            gout_full[hb * 256 : hb * 256 + 256, h * 128 : h * 128 + 128] = gout_ref[h, hb * 3 + 2].astype(F32)
-            gbias_ref[:, cols] = bout_ref[h, hb : hb + 1, :]
+            gin[:, cols] = gout_ref[h, hb * 2].astype(F32)
+            gfull[block, h * 128 : h * 128 + 128] = gout_ref[h, hb * 2 + 1].astype(F32)
+            for r in range(per):
+                piece = gz_ref[h, hb * per + r].astype(F32)
+                for z in range(zs):
+                    at = z * zq + r * zz
+                    gnet[at : at + zz, cols] = piece[z * zz : z * zz + zz]
+            gbias[:, cols] = bout_ref[h, hb : hb + 1, :]
+        put(gin.at[:, block], gin_ref.at[:, block])
+        put(gnet.at[:, block], gnet_ref.at[:, block])
+        put(gfull.at[block], gout_full.at[block])
+    put(gbias, gbias_ref)
+    for copy in copies:
+        copy.wait()
 
 
 def shape(dims, kind):
@@ -405,15 +502,18 @@
     hidden = w_in.shape[1]
     peers = 2 * nc // zs
     gr = 256 // peers
-    zr = 12 * gr // zs
+    zr = 8 * gr // zs
+    zq = 256 // zs
+    zz = 4 * zq // peers
     dma = pltpu.SemaphoreType.DMA
     vm = pltpu.VMEM
 
-    outs, gout, bout = pl.pallas_call(
+    outs, gout, gz, bout = pl.pallas_call(
         functools.partial(layer_kernel, nc, zs, slots),
-        out_shape=(shape((2, rows // 4, F), BF), shape((2, 12, 256, 128), BF), shape((2, 8, 128), F32)),
-        in_specs=[VM] * 6 + [ANY, ANY, VM, ANY],
-        out_specs=(VM, VM, VM),
+        out_shape=(shape((2, rows // 4, F), BF), shape((2, 8, peers // 4, 4, gr, 128), BF),
+                   shape((2, peers // 4, 4, zs * zz, 128), BF), shape((2, 8, 128), F32)),
+        in_specs=[VM] * 6 + [HBM, HBM, VM, HBM],
+        out_specs=(VM,) * 4,
         scratch_shapes=[
             vm((F, hidden), BF),
             vm((F, hidden), BF),
@@ -432,13 +532,15 @@
             vm((2, NETS, F), BF),
             vm((2, F, NETS), BF),
             vm((2, NETS, F), F32),
-            vm((2, 2, pins, F), F32),
-            vm((2, NETS, F), F32),
+            vm((pins, 5 * HB), BF),
+            vm((pins, 5 * HB), BF),
+            vm((NETS, 5 * HB), BF),
+            vm((2, 2 * pins, F), BF),
             vm((2, 16, 128), F32),
             vm((2, 12, 256, 128), F32),
             vm((12, 256, 128), F32),
             vm((12, 256, 128), BF),
-            vm((4, peers, 3, gr, 128), BF),
+            vm((4, peers, 2, gr, 128), BF),
             vm((16, 128), F32),
             vm((16, 128), BF),
             vm((peers, 16, 128), BF),
@@ -449,33 +551,40 @@
             vm((outer, F), BF),
             vm((outer, F), BF),
             vm((rows, F), F32),
-            vm((rows // 2, F), F32),
-            vm((rows // 2, F), BF),
+            vm((3, rows // 4, F), BF),
+            vm((rows, F), BF),
             vm((zs, zr + 8, 128), F32),
             vm((zs, zr + 8, 128), F32),
-            vm((zr, 128), F32),
-            vm((zs, zr, 128), F32),
-            vm((12, gr, 128), BF),
+            vm((zr + zz, 128), F32),
+            vm((zs, zr + zz, 128), F32),
+            vm((8, gr, 128), BF),
             vm((8, 128), F32),
+            vm((4, zs, zq, 128), BF),
+            vm((peers, zz, 128), F32),
+            vm((peers, zz, 128), F32),
+            vm((zs * zz, 128), BF),
             dma((3,)),
-            dma((23,)),
-            dma((23,)),
+            dma((33,)),
+            dma((33,)),
         ],
         compiler_params=pltpu.CompilerParams(collective_id=0, has_side_effects=True),
         name="layer",
-    )(cell_feat, out_grad, send_idx.reshape(nc, slots), pin_net.reshape(2, pins), pin_ref.reshape(2, pins),
+    )(cell_feat, out_grad, send_idx[0].T, pin_net.reshape(2, pins), pin_ref.reshape(2, pins),
       block_count, w_in, w_net, bias.reshape(1, hidden), w_out)
 
     updated, cell_grad, grad_in, grad_net, grad_bias, grad_out = pl.pallas_call(
-        finish_kernel,
+        functools.partial(finish_kernel, zs),
         out_shape=(
             shape((rows // 4, F), BF), shape((rows // 4, F), BF), shape((F, hidden), F32),
             shape((F, hidden), F32), shape((1, hidden), F32), shape((hidden, F), F32),
         ),
-        in_specs=[VM] * 3,
-        out_specs=(VM,) * 6,
+        in_specs=[VM] * 4,
+        out_specs=(ANY,) * 6,
+        scratch_shapes=[
+            vm((F, hidden), F32), vm((F, hidden), F32), vm((hidden, F), F32), vm((1, hidden), F32), dma((15,)),
+        ],
         name="finish",
-    )(outs, gout, bout)
+    )(outs, gout.reshape(2, 8, 256, 128), gz.reshape(2, peers, zs * zz, 128), bout)
     return (updated, cell_grad, grad_in, grad_net, grad_bias.reshape(hidden), grad_out)
 
 

time: 88.6 us -> 85 us (0.959); the launches traced: 87.3 us -> 84.8 us
  local copies, waits for them, and re-layouts: 1.39 us -> 0 us
  Pallas kernels: 84.6 us -> 83.5 us
    unnamed x1 -> x0, local copies, waits for them, and re-layouts: 1.39 us -> none
    pallas_call x1, Pallas kernels: 81.4 us -> 80.3 us  [local(): pl.pallas_call(functools.partial(layer_kernel, nc, zs, slots), out_shape=...]
where the time goes in v3:
time: 85 us; the launch traced here: 84.8 us
  Pallas kernels  83.5 us (98%)
  between operations  1.29 us (2%)
    pallas_call x1, Pallas kernels, local(): pl.pallas_call(functools.partial(layer_kernel, nc, zs, slots), out_shape=...  80.3 us
    pallas_call x1, Pallas kernels, local(): pl.pallas_call(functools.partial(finish_kernel, zs), out_shape=(shape((ro...  3.22 us

profile of v3, /device:TPU:1, one launch (start us, length us, event | category | flops | bytes accessed | tf_op | source)
XLA Modules:
  0.0 84.8 jit_solution(9559870220886225491)
XLA Ops:
  1.3 80.3 %layer.1 = (bf16[2,128,256]{2,1,0:T(8,128)(2,1)}, bf16[2,8,4,4,16,128]{5,4,3,2,1,0:T(8,128)(2,1)}, bf16[2,4,4,64,128]{4,3,2,1,0:T(8,128)(2,1)}, f32[2,8,128]{2,1,0:T(8,128)}) custom-call(bf16[512,256]{1,0:T(8,128)(2,1)} %x_ref.1, bf16[512,256]{1,0:T(8,128)(2,1)} %g_ref.1, s32[16,64]{1,0:T(8,128)} %bitcast.11, s32[2,512]{1,0:T(2,128)} %bitcast.12, ...), custom_call_target="tpu_custom_call" | custom-call | tf_op jit(solution)/shard_map/layer/pallas_call | solution.py:511
  81.6 3.2 %finish.1 = (bf16[128,256]{1,0:T(8,128)(2,1)}, bf16[128,256]{1,0:T(8,128)(2,1)}, f32[256,1024]{1,0:T(8,128)}, f32[256,1024]{1,0:T(8,128)}, f32[1,1024]{1,0:T(1,128)}, /*index=5*/f32[1024,256]{1,0:T(8,128)}) custom-call(bf16[2,128,256]{2,1,0:T(8,128)(2,1)} %get-tuple-element.16.outs_ref, bf16[2,8,256,128]{3,2,1,0:T(8,128)(2,1)} %bitcast.9, ...), custom_call_target="tpu_custom_call" | custom-call | tf_op jit(solution)/shard_map/finish/pallas_call | solution.py:575

commit v4 on v3

--- a/solution.py
+++ b/solution.py
@@ -18,7 +18,7 @@
 F32 = jnp.float32
 I32 = jnp.int32
 Z_SIZE = 8
-WAVES = (2, 2)
+WAVE = 2
 
 
 def dot(a, b, ca, cb):
@@ -54,7 +54,7 @@
                  w_in_ref, w_net_ref, w_out_ref, send_buf, halo, ids_buf, ids_recv, sel_t, gath, scat, pin, pin_xt,
                  into, onto, net_feat, net_feat_t, inv, hid, slope_g, net_g, vals, bsum, grads, grad_in, g_send, g_recv,
                  b_in, b_send, b_recv, far_buf, far_in, near_buf, near_in, a2a_buf, a2a_in, half_buf, half_in, fin,
-                 z_send, z_recv, z_fin, z_all, g_fin, b_fin, q_recv, r_send, r_recv, gz_fin, w_sem, send_sem, recv_sem):
+                 z_send, z_recv, bz_send, bz_recv, g_fin, q_recv, r_send, r_recv, r_fin, r_all, gz_fin, w_sem, send_sem, recv_sem):
     c = lax.axis_index("cell")
     n = lax.axis_index("net")
     core = lax.rem(n, 2)
@@ -65,7 +65,6 @@
     xy = nc // zs
     peers = 2 * xy
     gr = 256 // peers
-    zr = 8 * gr // zs
     zq = 256 // zs
     zz = 4 * zq // peers
     z = c // xy
@@ -277,6 +276,23 @@
         far_buf[k] = dot(scat[cells:, :], vals[k], 1, 0)
         near_buf[k] = dot(scat[0:cells, :], vals[k], 1, 0)
 
+    def over_z(buf, dst, i):
+        def push_z(k, _):
+            send(buf, dst.at[z], i, z_dev(lax.rem(z + k, zs)))
+            return 0
+
+        lax.fori_loop(1, zs, push_z, 0)
+        dst[z] = buf[...]
+
+    def reduce_z(hb):
+        arrived(g_recv.at[hb, pl.ds(0, peers - 1)], 7 + hb)
+        total = g_recv[hb, 0].astype(F32)
+        for k in range(1, peers):
+            total += g_recv[hb, k].astype(F32)
+        z_send[hb] = total.reshape(2 * gr, 128).astype(BF)
+        over_z(z_send.at[hb], z_recv.at[hb], 33 + hb)
+
+    reduce_z(0)
     scatter(other)
     send(far_buf.at[other], far_in, 12, near)
     send(near_buf.at[other], near_in, 13, near)
@@ -290,7 +306,9 @@
 
     lax.fori_loop(1, peers, push_b, 0)
     b_recv[p] = b_send[...]
+    reduce_z(1)
     scatter(core)
+    reduce_z(2)
 
     arrived(far_in, 12)
     a2a_buf[...] = (far_buf[core] + far_in[...]).astype(BF)
@@ -300,38 +318,20 @@
         send(a2a_buf.at[rows_at(d, slots)], a2a_in.at[mine], 15, (d, n))
         return 0
 
-    first = 1 + (nc - 1) * WAVES[0] // 8
-    second = first + (nc - 1) * WAVES[1] // 8
+    first = 1 + (nc - 1) * WAVE // 8
     lax.fori_loop(1, first, push_back, 0)
     a2a_in[mine, :] = a2a_buf[mine, :]
     arrived(near_in, 13)
     half_buf[...] = near_buf[core] + near_in[...]
-
-    part_sums = []
-    for hb in range(4):
-        arrived(g_recv.at[hb, pl.ds(0, peers - 1)], 7 + hb)
-        total = g_recv[hb, 0].astype(F32)
-        for k in range(1, peers):
-            total += g_recv[hb, k].astype(F32)
-        part_sums.append(total.reshape(2 * gr, 128))
-    flat = jnp.concatenate(part_sums, axis=0)
+    reduce_z(3)
+    lax.fori_loop(first, nc, push_back, 0)
+
     arrived(b_recv.at[pl.ds(0, peers - 1)], 14)
     b_sum = b_recv[0].astype(F32)
     for k in range(1, peers):
         b_sum += b_recv[k].astype(F32)
-    for k in range(zs):
-        z_send[k, 0:zr, :] = flat[k * zr : k * zr + zr, :]
-        z_send[k, zr : zr + 8, :] = b_sum[0:8, :]
-
-    def push_z(k, _):
-        t = lax.rem(z + k, zs)
-        send(z_send.at[t], z_recv.at[z], 16, z_dev(t))
-        return 0
-
-    lax.fori_loop(1, zs, push_z, 0)
-
-    lax.fori_loop(first, second, push_back, 0)
-    z_recv[z] = z_send[z]
+    bz_send[...] = b_sum[0:8, :]
+    over_z(bz_send, bz_recv, 16)
 
     q_sums = []
     for hb in range(4):
@@ -349,37 +349,23 @@
 
     lax.fori_loop(1, peers, push_r, 0)
     r_recv[p] = r_send[p]
-
-    arrived(z_recv.at[pl.ds(0, zs - 1)], 16)
-    zsum = z_recv[0]
-    for k in range(1, zs):
-        zsum += z_recv[k]
-    z_fin[0:zr, :] = zsum[0:zr, :]
-    b_fin[...] = zsum[zr : zr + 8, :]
     arrived(r_recv.at[pl.ds(0, peers - 1)], 29)
     rsum = r_recv[0]
     for k in range(1, peers):
         rsum += r_recv[k]
-    z_fin[zr : zr + zz, :] = rsum
-
-    def push_zg(k, _):
-        t = lax.rem(z + k, zs)
-        send(z_fin, z_all.at[z], 17, z_dev(t))
-        return 0
-
-    lax.fori_loop(1, zs, push_zg, 0)
-    lax.fori_loop(second, nc, push_back, 0)
-    z_all[z] = z_fin[...]
-    bout_ref[core] = b_fin[...]
-    send(b_fin, bout_ref.at[core], 18, near)
-
-    arrived(z_all.at[pl.ds(0, zs - 1)], 17)
-    g_fin[...] = z_all[:, 0:zr, :].reshape(8, gr, 128).astype(BF)
-    gz_fin[...] = z_all[:, zr : zr + zz, :].reshape(zs * zz, 128).astype(BF)
+    r_fin[...] = rsum
+
+    def push_ra(k, _):
+        send(r_fin, r_all.at[p], 17, xy_dev(lax.rem(p + k, peers)))
+        return 0
+
+    lax.fori_loop(1, peers, push_ra, 0)
+    r_all[p] = rsum
+
     xn = peers // 4
     x_at = p // 4
     y_at = lax.rem(p, 4)
-    one, two = pl.ds(0, 6), pl.ds(6, 2)
+    one, two = pl.ds(0, 4), pl.ds(4, 4)
 
     def to_x(k):
         return xy_dev(lax.rem(x_at + k, xn) * 4 + y_at)
@@ -387,22 +373,43 @@
     def to_y(k):
         return xy_dev(x_at * 4 + lax.rem(y_at + k, 4))
 
+    for hb in range(4):
+        arrived(z_recv.at[hb, pl.ds(0, zs - 1)], 33 + hb)
+        total = z_recv[hb, 0].astype(F32)
+        for k in range(1, zs):
+            total += z_recv[hb, k].astype(F32)
+        g_fin[2 * hb : 2 * hb + 2] = total.astype(BF).reshape(2, gr, 128)
     for k in range(1, xn):
         send(g_fin.at[one], gout_ref.at[core, one, x_at, y_at], 20, to_x(k))
     for k in range(1, 4):
         send(g_fin.at[two], gout_ref.at[core, two, x_at, y_at], 22, to_y(k))
-        send(gz_fin, gz_ref.at[core, x_at, y_at], 30, to_y(k))
     gout_ref[core, :, x_at, y_at] = g_fin[...]
-    gz_ref[core, x_at, y_at] = gz_fin[...]
+
+    arrived(r_all.at[pl.ds(0, peers - 1)], 17)
+    gz_fin[...] = r_all[...].reshape(4, zq, 128).astype(BF)
+    z_rows = rows_at(z, zq)
+
+    def push_gz(k, _):
+        send(gz_fin, gz_ref.at[core, :, z_rows, :], 30, z_dev(lax.rem(z + k, zs)))
+        return 0
+
+    lax.fori_loop(1, zs, push_gz, 0)
+    gz_ref[core, :, z_rows, :] = gz_fin[...]
+
     if xn > 1:
         arrived(gout_ref.at[core, one, pl.ds(0, xn - 1), 0], 20)
     for k in range(1, 4):
         send(gout_ref.at[core, one, :, y_at], gout_ref.at[core, one, :, y_at], 21, to_y(k))
     arrived(gout_ref.at[core, two, 0, pl.ds(0, 3)], 22)
-    arrived(gz_ref.at[core, 0, pl.ds(0, 3)], 30)
     for k in range(1, xn):
         send(gout_ref.at[core, two, x_at], gout_ref.at[core, two, x_at], 23, to_x(k))
-        send(gz_ref.at[core, x_at], gz_ref.at[core, x_at], 31, to_x(k))
+
+    arrived(bz_recv.at[pl.ds(0, zs - 1)], 16)
+    b_all = bz_recv[0]
+    for k in range(1, zs):
+        b_all += bz_recv[k]
+    bout_ref[core] = b_all
+    send(bout_ref.at[core], bout_ref.at[core], 18, near)
 
     arrived(a2a_in.at[most], 15)
     half_buf[...] += dot(sel_t[...], a2a_in[...], 1, 0)
@@ -411,6 +418,16 @@
     ours = rows_at(n, qr)
     for k, q in enumerate((mate, across, 3 - n)):
         send(fin.at[rows_at(q, qr)], half_in.at[k], 19, (c, q))
+
+    arrived(gout_ref.at[core, one, :, pl.ds(0, 3)], 21)
+    if xn > 1:
+        arrived(gout_ref.at[core, two, pl.ds(0, xn - 1)], 23)
+    send(gout_ref.at[core], gout_ref.at[core], 24, near)
+
+    zmost = gz_ref.at[core, :, pl.ds(0, (zs - 1) * zq), :]
+    arrived(zmost, 30)
+    send(gz_ref.at[core], gz_ref.at[core], 32, near)
+
     arrived(half_in, 19)
     kept = half_buf[ours, :] + half_in[1].astype(F32)
     swapped = half_in[0].astype(F32) + half_in[2].astype(F32)
@@ -418,14 +435,7 @@
     as_g = jnp.where(core == 0, swapped, kept)
     out_ref[0] = (as_x + x_ref[ours, :].astype(F32)).astype(BF)
     out_ref[1] = (as_g + g_ref[ours, :].astype(F32)).astype(BF)
-
-    arrived(gout_ref.at[core, one, :, pl.ds(0, 3)], 21)
-    if xn > 1:
-        arrived(gout_ref.at[core, two, pl.ds(0, xn - 1)], 23)
-        arrived(gz_ref.at[core, pl.ds(0, xn - 1)], 31)
-    send(gout_ref.at[core], gout_ref.at[core], 24, near)
-    send(gz_ref.at[core], gz_ref.at[core], 32, near)
-    arrived(b_fin, 18)
+    arrived(bout_ref.at[core], 18)
 
     left(halo.at[core, most], 0)
     left(ids_recv.at[pl.ds(0, 3)], 1)
@@ -434,35 +444,32 @@
         left(grad_in.at[pl.ds(hb * 3, 3)], 3 + hb)
         left(g_recv.at[hb, pl.ds(0, peers - 1)], 7 + hb)
         left(q_recv.at[hb, pl.ds(0, zs - 1)], 25 + hb)
+        left(z_recv.at[hb, pl.ds(0, zs - 1)], 33 + hb)
     left(b_in, 11)
     left(far_in, 12)
     left(near_in, 13)
     left(b_recv.at[pl.ds(0, peers - 1)], 14)
     left(a2a_in.at[most], 15)
-    left(z_recv.at[pl.ds(0, zs - 1)], 16)
-    left(z_all.at[pl.ds(0, zs - 1)], 17)
-    left(b_fin, 18)
+    left(bz_recv.at[pl.ds(0, zs - 1)], 16)
+    left(r_all.at[pl.ds(0, peers - 1)], 17)
+    left(bout_ref.at[core], 18)
     left(r_recv.at[pl.ds(0, peers - 1)], 29)
-    left(gz_ref.at[core, 0, pl.ds(0, 3)], 30)
+    left(zmost, 30)
     left(half_in, 19)
     left(gout_ref.at[core, one, :, pl.ds(0, 3)], 21)
     left(gout_ref.at[core, two, 0, pl.ds(0, 3)], 22)
     if xn > 1:
         left(gout_ref.at[core, one, pl.ds(0, xn - 1), 0], 20)
         left(gout_ref.at[core, two, pl.ds(0, xn - 1)], 23)
-        left(gz_ref.at[core, pl.ds(0, xn - 1)], 31)
     arrived(gout_ref.at[core], 24)
     left(gout_ref.at[core], 24)
     arrived(gz_ref.at[core], 32)
     left(gz_ref.at[core], 32)
 
 
-def finish_kernel(zs, outs_ref, gout_ref, gz_ref, bout_ref, y_ref, x_ref, gin_ref, gnet_ref, gbias_ref, gout_full,
+def finish_kernel(outs_ref, gout_ref, gz_ref, bout_ref, y_ref, x_ref, gin_ref, gnet_ref, gbias_ref, gout_full,
                   gin, gnet, gfull, gbias, sem):
     copies = []
-    zq = 256 // zs
-    zz = gz_ref.shape[2] // zs
-    per = gz_ref.shape[1] // 4
 
     def put(src, dst):
         copies.append(pltpu.make_async_copy(src, dst, sem.at[len(copies)]))
@@ -476,11 +483,7 @@
             cols = slice(hb * 256 + h * 128, hb * 256 + h * 128 + 128)
             gin[:, cols] = gout_ref[h, hb * 2].astype(F32)
             gfull[block, h * 128 : h * 128 + 128] = gout_ref[h, hb * 2 + 1].astype(F32)
-            for r in range(per):
-                piece = gz_ref[h, hb * per + r].astype(F32)
-                for z in range(zs):
-                    at = z * zq + r * zz
-                    gnet[at : at + zz, cols] = piece[z * zz : z * zz + zz]
+            gnet[:, cols] = gz_ref[h, hb].astype(F32)
             gbias[:, cols] = bout_ref[h, hb : hb + 1, :]
         put(gin.at[:, block], gin_ref.at[:, block])
         put(gnet.at[:, block], gnet_ref.at[:, block])
@@ -502,7 +505,6 @@
     hidden = w_in.shape[1]
     peers = 2 * nc // zs
     gr = 256 // peers
-    zr = 8 * gr // zs
     zq = 256 // zs
     zz = 4 * zq // peers
     dma = pltpu.SemaphoreType.DMA
@@ -511,7 +513,7 @@
     outs, gout, gz, bout = pl.pallas_call(
         functools.partial(layer_kernel, nc, zs, slots),
         out_shape=(shape((2, rows // 4, F), BF), shape((2, 8, peers // 4, 4, gr, 128), BF),
-                   shape((2, peers // 4, 4, zs * zz, 128), BF), shape((2, 8, 128), F32)),
+                   shape((2, 4, 256, 128), BF), shape((2, 8, 128), F32)),
         in_specs=[VM] * 6 + [HBM, HBM, VM, HBM],
         out_specs=(VM,) * 4,
         scratch_shapes=[
@@ -553,27 +555,32 @@
             vm((rows, F), F32),
             vm((3, rows // 4, F), BF),
             vm((rows, F), BF),
-            vm((zs, zr + 8, 128), F32),
-            vm((zs, zr + 8, 128), F32),
-            vm((zr + zz, 128), F32),
-            vm((zs, zr + zz, 128), F32),
+            vm((4, 2 * gr, 128), BF),
+            vm((4, zs, 2 * gr, 128), BF),
+            vm((8, 128), F32),
+            vm((zs, 8, 128), F32),
             vm((8, gr, 128), BF),
-            vm((8, 128), F32),
             vm((4, zs, zq, 128), BF),
             vm((peers, zz, 128), F32),
             vm((peers, zz, 128), F32),
-            vm((zs * zz, 128), BF),
+            vm((zz, 128), F32),
+            vm((peers, zz, 128), F32),
+            vm((4, zq, 128), BF),
             dma((3,)),
-            dma((33,)),
-            dma((33,)),
+            dma((37,)),
+            dma((37,)),
         ],
-        compiler_params=pltpu.CompilerParams(collective_id=0, has_side_effects=True),
+        compiler_params=pltpu.CompilerParams(collective_id=0, has_side_effects=True, vmem_limit_bytes=48 << 20),
         name="layer",
-    )(cell_feat, out_grad, send_idx[0].T, pin_net.reshape(2, pins), pin_ref.reshape(2, pins),
-      block_count, w_in, w_net, bias.reshape(1, hidden), w_out)
+    )(*[
+        pltpu.with_memory_space_constraint(v, pltpu.HBM)
+        for v in (cell_feat, out_grad, send_idx[0].T, pin_net.reshape(2, pins), pin_ref.reshape(2, pins))
+    ], block_count, *[
+        pltpu.with_memory_space_constraint(v, pltpu.HBM) for v in (w_in, w_net, bias.reshape(1, hidden), w_out)
+    ])
 
     updated, cell_grad, grad_in, grad_net, grad_bias, grad_out = pl.pallas_call(
-        functools.partial(finish_kernel, zs),
+        finish_kernel,
         out_shape=(
             shape((rows // 4, F), BF), shape((rows // 4, F), BF), shape((F, hidden), F32),
             shape((F, hidden), F32), shape((1, hidden), F32), shape((hidden, F), F32),
@@ -583,8 +590,9 @@
         scratch_shapes=[
             vm((F, hidden), F32), vm((F, hidden), F32), vm((hidden, F), F32), vm((1, hidden), F32), dma((15,)),
         ],
+        compiler_params=pltpu.CompilerParams(vmem_limit_bytes=12 << 20),
         name="finish",
-    )(outs, gout.reshape(2, 8, 256, 128), gz.reshape(2, peers, zs * zz, 128), bout)
+    )(outs, gout.reshape(2, 8, 256, 128), gz, bout)
     return (updated, cell_grad, grad_in, grad_net, grad_bias.reshape(hidden), grad_out)
 
 

time: 85 us -> 74.8 us (0.88)
  Pallas kernels: 83.5 us -> 73.4 us
    pallas_call x1, Pallas kernels: 80.3 us -> 71.6 us  [local(): pl.pallas_call(functools.partial(layer_kernel, nc, zs, slots), out_shape=...]
    pallas_call x1, Pallas kernels: 3.22 us -> 1.83 us  [local(): pl.pallas_call(finish_kernel, out_shape=(shape((rows // 4, F), BF), shape...]
where the time goes in v4:
time: 74.8 us; the launch traced here: 74.7 us
  Pallas kernels  73.4 us (98%)
  between operations  1.29 us (2%)
    pallas_call x1, Pallas kernels, local(): pl.pallas_call(functools.partial(layer_kernel, nc, zs, slots), out_shape=...  71.6 us
    pallas_call x1, Pallas kernels, local(): pl.pallas_call(finish_kernel, out_shape=(shape((rows // 4, F), BF), shape...  1.83 us

profile of v4, /device:TPU:1, one launch (start us, length us, event | category | flops | bytes accessed | tf_op | source)
XLA Modules:
  0.0 74.7 jit_solution(17639474538473897780)
XLA Ops:
  1.3 71.6 %layer.1 = (bf16[2,128,256]{2,1,0:T(8,128)(2,1)S(1)}, bf16[2,8,4,4,16,128]{5,4,3,2,1,0:T(8,128)(2,1)S(1)}, bf16[2,4,256,128]{3,2,1,0:T(8,128)(2,1)S(1)}, f32[2,8,128]{2,1,0:T(8,128)S(1)}) custom-call(bf16[512,256]{1,0:T(8,128)(2,1)} %x_ref.1, bf16[512,256]{1,0:T(8,128)(2,1)} %g_ref.1, s32[16,64]{1,0:T(8,128)} %bitcast.9, s32[2,512]{1,0:T(2,128)} %bitcast.10, ...), custom_call_target="tpu_custom_call" | custom-call | tf_op jit(solution)/shard_map/layer/pallas_call | solution.py:513
  72.9 1.8 %finish.1 = (bf16[128,256]{1,0:T(8,128)(2,1)}, bf16[128,256]{1,0:T(8,128)(2,1)}, f32[256,1024]{1,0:T(8,128)}, f32[256,1024]{1,0:T(8,128)}, f32[1,1024]{1,0:T(1,128)}, /*index=5*/f32[1024,256]{1,0:T(8,128)}) custom-call(bf16[2,128,256]{2,1,0:T(8,128)(2,1)S(1)} %get-tuple-element.16.outs_ref, bf16[2,8,256,128]{3,2,1,0:T(8,128)(2,1)S(1)} %bitcast.8, ...), custom_call_target="tpu_custom_call" | custom-call | tf_op jit(solution)/shard_map/finish/pallas_call | solution.py:582

commit v5 on v4

--- a/solution.py
+++ b/solution.py
@@ -49,9 +49,9 @@
 
 
 def layer_kernel(nc, zs, slots,
-                 x_ref, g_ref, idx_ref, net_ref, ref_ref, cnt_ref, w_in_hbm, w_net_hbm, bias_ref, w_out_hbm,
+                 x_hbm, g_hbm, idx_hbm, net_hbm, ref_hbm, cnt_ref, w_in_hbm, w_net_hbm, bias_hbm, w_out_hbm,
                  out_ref, gout_ref, gz_ref, bout_ref,
-                 w_in_ref, w_net_ref, w_out_ref, send_buf, halo, ids_buf, ids_recv, sel_t, gath, scat, pin, pin_xt,
+                 x_ref, g_ref, idx_ref, net_ref, ref_ref, bias_ref, w_in_ref, w_net_ref, w_out_ref, send_buf, halo, ids_buf, ids_recv, sel_t, gath, scat, pin, pin_xt,
                  into, onto, net_feat, net_feat_t, inv, hid, slope_g, net_g, vals, bsum, grads, grad_in, g_send, g_recv,
                  b_in, b_send, b_recv, far_buf, far_in, near_buf, near_in, a2a_buf, a2a_in, half_buf, half_in, fin,
                  z_send, z_recv, bz_send, bz_recv, g_fin, q_recv, r_send, r_recv, r_fin, r_all, gz_fin, w_sem, send_sem, recv_sem):
@@ -74,6 +74,15 @@
     cells = x_ref.shape[0]
     outer = nc * slots
     pins = ref_ref.shape[1]
+    loads = [
+        pltpu.make_async_copy(src, dst, w_sem.at[i])
+        for i, (src, dst) in enumerate((
+            (idx_hbm, idx_ref), (x_hbm, x_ref), (g_hbm, g_ref), (net_hbm, net_ref), (ref_hbm, ref_ref),
+            (bias_hbm, bias_ref), (w_in_hbm, w_in_ref), (w_net_hbm, w_net_ref), (w_out_hbm, w_out_ref),
+        ))
+    ]
+    for load in loads:
+        load.start()
     sem = lambda i: (send_sem.at[i], recv_sem.at[i])
 
     def send(src, dst, i, dev):
@@ -112,13 +121,8 @@
     hail(near)
     hail((c, 3 - n))
 
-    loads = [
-        pltpu.make_async_copy(src, dst, w_sem.at[i])
-        for i, (src, dst) in enumerate(((w_in_hbm, w_in_ref), (w_net_hbm, w_net_ref), (w_out_hbm, w_out_ref)))
-    ]
-    for load in loads:
-        load.start()
-
+    for load in loads[:5]:
+        load.wait()
     idx = idx_ref[...]
     high = (idx // 2).astype(F32).astype(BF)
     low = lax.rem(idx, 2).astype(F32).astype(BF)
@@ -137,15 +141,32 @@
 
     mine = rows_at(c, slots)
 
+    lanes, relay_lanes = pl.ds(0, 128), pl.ds(128, 128)
+    relays = lax.rem(z, 2) == y_hi
+
+    @pl.when(relays)
+    def _():
+        def push_relay(k, _):
+            d = lax.rem(c + k, nc)
+            send(send_buf.at[rows_at(d, slots), relay_lanes], halo.at[core, mine, relay_lanes], 37, (d, n))
+            return 0
+
+        lax.fori_loop(1, nc, push_relay, 0)
+
     def push(k, _):
         d = lax.rem(c + k, nc)
-        send(send_buf.at[rows_at(d, slots)], halo.at[core, mine], 0, (d, n))
+        send(send_buf.at[rows_at(d, slots), lanes], halo.at[core, mine, lanes], 0, (d, n))
         return 0
 
     lax.fori_loop(1, nc, push, 0)
     for m in range(1, 4):
         send(ids_buf, ids_recv.at[n], 1, (c, lax.rem(n + m, 4)))
-    halo[core, mine, :] = send_buf[mine, :]
+    halo[core, mine, 0:128] = send_buf[mine, 0:128]
+
+    @pl.when(relays)
+    def _():
+        halo[core, mine, 128:256] = send_buf[mine, 128:256]
+
     ids_recv[n] = ids_buf[...]
 
     def lists(b, refs, nets):
@@ -165,14 +186,28 @@
     bsum[...] = jnp.zeros_like(bsum)
     arrived(ids_recv.at[pl.ds(0, 3)], 1)
     ids = ids_recv[0] + ids_recv[1] + ids_recv[2] + ids_recv[3]
+    some = outer // 2
+
+    @pl.when(relays)
+    def _():
+        arrived(halo.at[core, pl.ds(0, some - slots), relay_lanes], 37)
+
+    @pl.when(jnp.logical_not(relays))
+    def _():
+        arrived(halo.at[core, pl.ds(0, some), relay_lanes], 37)
+
+    for k in range(zs // 2):
+        plane = halo.at[core, rows_at(y_hi + 2 * k, xy * slots), relay_lanes]
+        send(plane, plane, 38, (c, across))
     lists(1, ids[0:1, :], ids[1:2, :])
     idx_row = jnp.broadcast_to(idx_col.astype(F32), (outer, 8)).T[0:1, :].astype(I32)
     sel_t[...] = ones_where(iota((cells, outer), 0) == idx_row)
-    for load in loads:
+    for load in loads[5:]:
         load.wait()
 
     most = pl.ds(0, (nc - 1) * slots)
-    arrived(halo.at[core, most], 0)
+    arrived(halo.at[core, most, lanes], 0)
+    arrived(halo.at[core, pl.ds(0, some), relay_lanes], 38)
     send(halo.at[core], halo.at[core], 2, near)
 
     def fetch(k):
@@ -437,7 +472,13 @@
     out_ref[1] = (as_g + g_ref[ours, :].astype(F32)).astype(BF)
     arrived(bout_ref.at[core], 18)
 
-    left(halo.at[core, most], 0)
+    left(halo.at[core, most, lanes], 0)
+    left(halo.at[core, pl.ds(0, some), relay_lanes], 38)
+
+    @pl.when(relays)
+    def _():
+        left(halo.at[core, most, relay_lanes], 37)
+
     left(ids_recv.at[pl.ds(0, 3)], 1)
     left(halo.at[core], 2)
     for hb in range(4):
@@ -514,9 +555,15 @@
         functools.partial(layer_kernel, nc, zs, slots),
         out_shape=(shape((2, rows // 4, F), BF), shape((2, 8, peers // 4, 4, gr, 128), BF),
                    shape((2, 4, 256, 128), BF), shape((2, 8, 128), F32)),
-        in_specs=[VM] * 6 + [HBM, HBM, VM, HBM],
+        in_specs=[HBM] * 5 + [VM] + [HBM] * 4,
         out_specs=(VM,) * 4,
         scratch_shapes=[
+            vm((rows, F), BF),
+            vm((rows, F), BF),
+            vm((slots, nc), I32),
+            vm((2, pins), I32),
+            vm((2, pins), I32),
+            vm((1, hidden), F32),
             vm((F, hidden), BF),
             vm((F, hidden), BF),
             vm((hidden, F), BF),
@@ -566,9 +613,9 @@
             vm((zz, 128), F32),
             vm((peers, zz, 128), F32),
             vm((4, zq, 128), BF),
-            dma((3,)),
-            dma((37,)),
-            dma((37,)),
+            dma((9,)),
+            dma((39,)),
+            dma((39,)),
         ],
         compiler_params=pltpu.CompilerParams(collective_id=0, has_side_effects=True, vmem_limit_bytes=48 << 20),
         name="layer",

time: 74.8 us -> 72.9 us (0.975)
  Pallas kernels: 73.4 us -> 71.5 us
    pallas_call x1, Pallas kernels: 71.6 us -> 69.7 us  [local(): pl.pallas_call(functools.partial(layer_kernel, nc, zs, slots), out_shape=...]
where the time goes in v5:
time: 72.9 us; the launch traced here: 72.8 us
  Pallas kernels  71.5 us (98%)
  between operations  1.29 us (2%)
    pallas_call x1, Pallas kernels, local(): pl.pallas_call(functools.partial(layer_kernel, nc, zs, slots), out_shape=...  69.7 us
    pallas_call x1, Pallas kernels, local(): pl.pallas_call(finish_kernel, out_shape=(shape((rows // 4, F), BF), shape...  1.83 us

profile of v5, /device:TPU:1, one launch (start us, length us, event | category | flops | bytes accessed | tf_op | source)
XLA Modules:
  0.0 72.8 jit_solution(17091769196331989328)
XLA Ops:
  1.3 69.7 %layer.1 = (bf16[2,128,256]{2,1,0:T(8,128)(2,1)S(1)}, bf16[2,8,4,4,16,128]{5,4,3,2,1,0:T(8,128)(2,1)S(1)}, bf16[2,4,256,128]{3,2,1,0:T(8,128)(2,1)S(1)}, f32[2,8,128]{2,1,0:T(8,128)S(1)}) custom-call(bf16[512,256]{1,0:T(8,128)(2,1)} %x_hbm.1, bf16[512,256]{1,0:T(8,128)(2,1)} %g_hbm.1, s32[16,64]{1,0:T(8,128)} %bitcast.9, s32[2,512]{1,0:T(2,128)} %bitcast.10, ...), custom_call_target="tpu_custom_call" | custom-call | tf_op jit(solution)/shard_map/layer/pallas_call | solution.py:554
  71.0 1.8 %finish.1 = (bf16[128,256]{1,0:T(8,128)(2,1)}, bf16[128,256]{1,0:T(8,128)(2,1)}, f32[256,1024]{1,0:T(8,128)}, f32[256,1024]{1,0:T(8,128)}, f32[1,1024]{1,0:T(1,128)}, /*index=5*/f32[1024,256]{1,0:T(8,128)}) custom-call(bf16[2,128,256]{2,1,0:T(8,128)(2,1)S(1)} %get-tuple-element.16.outs_ref, bf16[2,8,256,128]{3,2,1,0:T(8,128)(2,1)S(1)} %bitcast.8, ...), custom_call_target="tpu_custom_call" | custom-call | tf_op jit(solution)/shard_map/finish/pallas_call | solution.py:629

commit v6 on v5

--- a/solution.py
+++ b/solution.py
@@ -18,7 +18,7 @@
 F32 = jnp.float32
 I32 = jnp.int32
 Z_SIZE = 8
-WAVE = 2
+WAVE = 1
 
 
 def dot(a, b, ca, cb):
@@ -207,15 +207,17 @@
 
     most = pl.ds(0, (nc - 1) * slots)
     arrived(halo.at[core, most, lanes], 0)
+    send(halo.at[core, :, lanes], halo.at[core, :, lanes], 2, near)
     arrived(halo.at[core, pl.ds(0, some), relay_lanes], 38)
-    send(halo.at[core], halo.at[core], 2, near)
+    send(halo.at[core, :, relay_lanes], halo.at[core, :, relay_lanes], 39, near)
 
     def fetch(k):
         for b in range(2):
             pin[k, b] += dot(gath[b, :, cells:], halo[k], 1, 0).astype(BF)
 
     fetch(core)
-    arrived(halo.at[core], 2)
+    arrived(halo.at[core, :, lanes], 2)
+    arrived(halo.at[core, :, relay_lanes], 39)
     fetch(other)
 
     for b in range(2):
@@ -307,8 +309,10 @@
         vals[1, mine_b, :] = (dot(slope_g[:, cols], w_in, 1, 1) + dot(onto[b], feat_grad, 1, 0)).astype(BF)
     spread_grads(3)
 
-    def scatter(k):
+    def scatter_far(k):
         far_buf[k] = dot(scat[cells:, :], vals[k], 1, 0)
+
+    def scatter_near(k):
         near_buf[k] = dot(scat[0:cells, :], vals[k], 1, 0)
 
     def over_z(buf, dst, i):
@@ -327,9 +331,10 @@
         z_send[hb] = total.reshape(2 * gr, 128).astype(BF)
         over_z(z_send.at[hb], z_recv.at[hb], 33 + hb)
 
+    scatter_far(other)
+    send(far_buf.at[other], far_in, 12, near)
     reduce_z(0)
-    scatter(other)
-    send(far_buf.at[other], far_in, 12, near)
+    scatter_near(other)
     send(near_buf.at[other], near_in, 13, near)
     arrived(b_in, 11)
     b_send[...] = (bsum[core] + b_in[...]).astype(BF)
@@ -342,9 +347,8 @@
     lax.fori_loop(1, peers, push_b, 0)
     b_recv[p] = b_send[...]
     reduce_z(1)
-    scatter(core)
+    scatter_far(core)
     reduce_z(2)
-
     arrived(far_in, 12)
     a2a_buf[...] = (far_buf[core] + far_in[...]).astype(BF)
 
@@ -356,10 +360,11 @@
     first = 1 + (nc - 1) * WAVE // 8
     lax.fori_loop(1, first, push_back, 0)
     a2a_in[mine, :] = a2a_buf[mine, :]
+    reduce_z(3)
+    lax.fori_loop(first, nc, push_back, 0)
+    scatter_near(core)
     arrived(near_in, 13)
     half_buf[...] = near_buf[core] + near_in[...]
-    reduce_z(3)
-    lax.fori_loop(first, nc, push_back, 0)
 
     arrived(b_recv.at[pl.ds(0, peers - 1)], 14)
     b_sum = b_recv[0].astype(F32)
@@ -439,13 +444,6 @@
     for k in range(1, xn):
         send(gout_ref.at[core, two, x_at], gout_ref.at[core, two, x_at], 23, to_x(k))
 
-    arrived(bz_recv.at[pl.ds(0, zs - 1)], 16)
-    b_all = bz_recv[0]
-    for k in range(1, zs):
-        b_all += bz_recv[k]
-    bout_ref[core] = b_all
-    send(bout_ref.at[core], bout_ref.at[core], 18, near)
-
     arrived(a2a_in.at[most], 15)
     half_buf[...] += dot(sel_t[...], a2a_in[...], 1, 0)
     fin[...] = half_buf[...].astype(BF)
@@ -453,6 +451,13 @@
     ours = rows_at(n, qr)
     for k, q in enumerate((mate, across, 3 - n)):
         send(fin.at[rows_at(q, qr)], half_in.at[k], 19, (c, q))
+
+    arrived(bz_recv.at[pl.ds(0, zs - 1)], 16)
+    b_all = bz_recv[0]
+    for k in range(1, zs):
+        b_all += bz_recv[k]
+    bout_ref[core] = b_all
+    send(bout_ref.at[core], bout_ref.at[core], 18, near)
 
     arrived(gout_ref.at[core, one, :, pl.ds(0, 3)], 21)
     if xn > 1:
@@ -480,7 +485,8 @@
         left(halo.at[core, most, relay_lanes], 37)
 
     left(ids_recv.at[pl.ds(0, 3)], 1)
-    left(halo.at[core], 2)
+    left(halo.at[core, :, lanes], 2)
+    left(halo.at[core, :, relay_lanes], 39)
     for hb in range(4):
         left(grad_in.at[pl.ds(hb * 3, 3)], 3 + hb)
         left(g_recv.at[hb, pl.ds(0, peers - 1)], 7 + hb)
@@ -614,8 +620,8 @@
             vm((peers, zz, 128), F32),
             vm((4, zq, 128), BF),
             dma((9,)),
-            dma((39,)),
-            dma((39,)),
+            dma((40,)),
+            dma((40,)),
         ],
         compiler_params=pltpu.CompilerParams(collective_id=0, has_side_effects=True, vmem_limit_bytes=48 << 20),
         name="layer",

time: 72.9 us -> 72.7 us (level)
  no operation moved by 1% of the time
where the time goes in v6:
time: 72.7 us; the launch traced here: 72.6 us
  Pallas kernels  71.3 us (98%)
  between operations  1.29 us (2%)
    pallas_call x1, Pallas kernels, local(): pl.pallas_call(functools.partial(layer_kernel, nc, zs, slots), out_shape=...  69.5 us
    pallas_call x1, Pallas kernels, local(): pl.pallas_call(finish_kernel, out_shape=(shape((rows // 4, F), BF), shape...  1.83 us

profile of v6, /device:TPU:1, one launch (start us, length us, event | category | flops | bytes accessed | tf_op | source)
XLA Modules:
  0.0 72.6 jit_solution(2700905281089985652)
XLA Ops:
  1.3 69.5 %layer.1 = (bf16[2,128,256]{2,1,0:T(8,128)(2,1)S(1)}, bf16[2,8,4,4,16,128]{5,4,3,2,1,0:T(8,128)(2,1)S(1)}, bf16[2,4,256,128]{3,2,1,0:T(8,128)(2,1)S(1)}, f32[2,8,128]{2,1,0:T(8,128)S(1)}) custom-call(bf16[512,256]{1,0:T(8,128)(2,1)} %x_hbm.1, bf16[512,256]{1,0:T(8,128)(2,1)} %g_hbm.1, s32[16,64]{1,0:T(8,128)} %bitcast.9, s32[2,512]{1,0:T(2,128)} %bitcast.10, ...), custom_call_target="tpu_custom_call" | custom-call | tf_op jit(solution)/shard_map/layer/pallas_call | solution.py:560
  70.8 1.8 %finish.1 = (bf16[128,256]{1,0:T(8,128)(2,1)}, bf16[128,256]{1,0:T(8,128)(2,1)}, f32[256,1024]{1,0:T(8,128)}, f32[256,1024]{1,0:T(8,128)}, f32[1,1024]{1,0:T(1,128)}, /*index=5*/f32[1024,256]{1,0:T(8,128)}) custom-call(bf16[2,128,256]{2,1,0:T(8,128)(2,1)S(1)} %get-tuple-element.16.outs_ref, bf16[2,8,256,128]{3,2,1,0:T(8,128)(2,1)S(1)} %bitcast.8, ...), custom_call_target="tpu_custom_call" | custom-call | tf_op jit(solution)/shard_map/finish/pallas_call | solution.py:635
